TPU v7x, 256 devices: a whole 4x4x8 slice. The times are simulated.
256 devices in a mesh: row: 16 (over z, x_hi), col: 16 (over y, x_lo, core).
Axes of the slice: x: 4 (x_hi: 2, x_lo: 2; x = x_hi * 2 + x_lo), y: 4, z: 8, core: 2. Of those that a mesh axis runs over, the one named last changes fastest.
Arguments:
- amplitudes: bfloat16 [8192, 8192], P('row', 'col'), may hold values from -6 to 6
- integrals: bfloat16 [8192, 8192], P('col', 'row'), may hold values from -0.09375 to 0.09375
- base_residual: float32 [8192, 8192], P('row', 'col'), may hold values from -6 to 6
- inv_denominators: float32 [8192, 8192], P('row', 'col'), may hold values from 0.1 to 0.5
- amp_mask: int32 [32, 32], P('row', 'col'), may hold values 0 or 1
- int_mask: int32 [32, 32], P('col', 'row'), may hold values 0 or 1
- res_mask: int32 [32, 32], P('row', 'col'), may hold values 0 or 1
Outputs:
- new_amplitudes: bfloat16 [8192, 8192], P('row', 'col')
- residual: float32 [8192, 8192], P('row', 'col')
Inputs may be any that keep to these rules, and one draw needn't show every extreme that they name: `amp_mask`: tile kept (1) or dropped (0). `int_mask`: tile kept (1) or dropped (0). `res_mask`: tile kept (1) or dropped (0).
All inputs are finite; a program needn't handle non-finite values. No bound on the sum of `amp_mask` or of `int_mask` or of `res_mask` on one device may be relied on, other than what follows from the above.
Results may differ from a plain program's by a relative error of at most 0.012.
Values may be sent and summed in bfloat16 or wider, within the bound.
No kernel may reach another device: no remote copies, remote signals or barrier semaphores. Data moves between devices by JAX's collectives and lax.ppermute only.
A program may use at most 128 MiB of HBM per device.

v0:
```python
import functools

import jax
import jax.numpy as jnp
from jax import lax
from jax.experimental import pallas as pl
from jax.experimental.pallas import tpu as pltpu
from jax.sharding import Mesh
from jax.sharding import PartitionSpec as P

AX = ("xh", "xl", "c")
BF = jnp.bfloat16
F32 = jnp.float32
LIMIT = 24 << 20
ROWS = 512
VM = pl.BlockSpec(memory_space=pltpu.VMEM)
SM = pl.BlockSpec(memory_space=pltpu.SMEM)
ANY = pl.BlockSpec(memory_space=pl.ANY)


def shape(*dims, dtype=BF):
    return jax.ShapeDtypeStruct(dims, dtype)


def permute_x(value, move):
    pairs = []
    for xh in range(2):
        for xl in range(2):
            for c in range(2):
                th, tl, tc = move(xh, xl, c)
                pairs.append((xh * 4 + xl * 2 + c, th * 4 + tl * 2 + tc))
    return lax.ppermute(value, AX, pairs)


def chip_xor(value, j):
    return permute_x(value, lambda xh, xl, c: (xh ^ (j >> 1), xl ^ (j & 1), c))


def core_swap(value):
    return permute_x(value, lambda xh, xl, c: (xh, xl, 1 - c))


def shift_z(value, s):
    return lax.ppermute(value, "z", [(i, (i + s) % 8) for i in range(8)])


def xor_y(value, t):
    return lax.ppermute(value, "y", [(i, i ^ t) for i in range(4)])


def call(body, outs, in_specs, out_specs, flops=0, moved=1 << 20, **kw):
    return pl.pallas_call(
        body,
        out_shape=outs,
        in_specs=in_specs,
        out_specs=out_specs,
        cost_estimate=pl.CostEstimate(flops=flops, bytes_accessed=moved, transcendentals=0),
        compiler_params=pltpu.CompilerParams(vmem_limit_bytes=LIMIT),
        **kw,
    )


def kept(idx, which, r, s):
    return (idx[r, s] >> which) & 1


def placed(idx):
    place = idx[0, 0] >> 3
    return [(place >> at) & size for at, size in ((0, 3), (2, 1), (1, 1), (0, 1), (3, 7), (6, 3))]


AMASK, IMASK, RMASK = 0, 1, 2


def lanes(q):
    return pl.ds(pl.multiple_of(q * 128, 128), 128)


def prep_w(idx, ints, *outs):
    _, c, _, xl, _, _ = placed(idx)
    for a in range(2):
        for b in range(2):
            col = c ^ a
            for r in range(2):
                keep = kept(idx, IMASK, r, col).astype(BF)
                outs[a * 2 + b][r * 256 : r * 256 + 256] = ints[r * 256 : r * 256 + 256, lanes(col * 2 + (xl ^ b))] * keep


def join_w(low, high, out):
    out[:512] = low[...]
    out[512:] = high[...]


def join_a(zero, one, two, three, out):
    out[0] = zero[...]
    out[1] = one[...]
    out[2] = two[...]
    out[3] = three[...]


def prep_a(idx, amps, masked):
    for r in range(2):
        for s in range(2):
            tile = (slice(r * 256, r * 256 + 256), slice(s * 256, s * 256 + 256))
            masked[tile] = amps[tile] * kept(idx, AMASK, r, s).astype(BF)


def prep_t(idx, base, invd, *outs):
    d = placed(idx)[0]
    for r in range(2):
        rows = slice(r * 256, r * 256 + 256)
        for j in range(4):
            q = d ^ j
            keep = (kept(idx, AMASK, r, q >> 1) * kept(idx, RMASK, r, q >> 1)).astype(F32)
            outs[j][0, rows] = base[rows, lanes(q)].astype(BF)
            outs[j][1, rows] = (invd[rows, lanes(q)] * keep).astype(BF)


EVEN = ((0, 1), (6, 7), (2, 3), (4, 5))
ODD = ((7, 0), (1, 2), (5, 6), (3, 4))


def first_kernel(ks, count, idx, *refs):
    pairs = [refs[8 * i : 8 * i + 8] for i in range(len(ks))]
    refs = refs[8 * len(ks) :]
    left, rest = refs[:4], refs[4]
    sends, wv, outv, osem = (lambda r: (r[:4], *r[4:]))(refs[5 + count :])
    _, c, xh, _, z, y = placed(idx)
    odd_z = z & 1
    flip = c ^ xh
    dests = [(z // 2 + (0, 3 - odd_z * 2, 1 + odd_z * 2, 2)[k]) & 3 for k in ks]

    def store(i, t):
        return pltpu.make_async_copy(outv.at[i], sends[t], osem.at[i])

    for i in range(len(ks)):
        for odd in range(2):

            @pl.when(odd_z == odd)
            def _(i=i, odd=odd):
                for e in range(2):
                    for a in range(2):
                        wv[a, :, e * 128 : e * 128 + 128] = pairs[i][odd * 4 + e * 2 + a][...]

        for half in range(2):
            own = jnp.concatenate([left[half * 2][...], left[half * 2 + 1][...]], 1)
            other = jnp.concatenate([rest[half * 2], rest[half * 2 + 1]], 1)
            total = jnp.dot(own, wv[flip], preferred_element_type=F32)
            total += jnp.dot(other, wv[1 - flip], preferred_element_type=F32)
            outv[i, xh ^ half] = total.astype(BF)
        for t in range(4):

            @pl.when((dests[i] ^ y) == t)
            def _(i=i, t=t):
                store(i, t).start()

    for i in range(len(ks)):
        store(i, 0).wait()


def first_product(ks, idx, pieces, left, carried):
    group = [pieces[a][s] for k in ks for pairs in (EVEN[k], ODD[k]) for s in pairs for a in range(2)]
    return call(
        functools.partial(first_kernel, ks, len(carried)),
        [shape(2, 512, 256)] * 4,
        [SM] + [VM] * len(group) + [VM] * 5 + [ANY] * len(carried),
        [ANY] * 4,
        flops=len(ks) * 2 * 1024 * 2048 * 256,
        moved=len(ks) << 20,
        scratch_shapes=[
            pltpu.VMEM((2, 1024, 256), BF),
            pltpu.VMEM((len(ks), 2, 512, 256), BF),
            pltpu.SemaphoreType.DMA((len(ks),)),
        ],
        input_output_aliases={6 + len(group) + i: i for i in range(len(carried))},
    )(idx, *group, *left, *carried)


def arrange(idx, *refs):
    d, c, xh, xl, z, _ = placed(idx)
    out = refs[16]
    for a in range(2):
        for s in range(8):
            piece = refs[a * 8 + s]
            owner = (z + s) & 7

            @pl.loop(0, 8)
            def _(block, a=a, piece=piece, owner=owner):
                e, q = block >> 2, block & 3
                at = (((a ^ c ^ xh) * 4 + (q ^ d)) * 2 + (e ^ xl)) * 128
                rows = pl.ds(pl.multiple_of(at, 128), 128)
                out[owner >> 1, rows, lanes(owner & 1)] = piece[pl.ds(pl.multiple_of(block * 128, 128), 128)]


def second_kernel(order, idx, *refs):
    left, weights, outs = refs[:8], refs[8], refs[9:]

    @pl.loop(0, 2)
    def _(h):
        whole = jnp.concatenate([ref[h] for ref in left], 1)
        got = jnp.dot(whole, weights[...], preferred_element_type=F32).astype(BF)
        for i in range(len(order)):

            @pl.when(pl.program_id(0) == i)
            def _(i=i):
                outs[i][h] = got


def second_product(t, idx, left, w_all):
    order = (t,)
    whole = pl.BlockSpec((2, ROWS, 256), lambda i, s: (0, 0, 0))
    return pl.pallas_call(
        functools.partial(second_kernel, order),
        out_shape=[shape(2, ROWS, 256)] * len(order),
        grid_spec=pltpu.PrefetchScalarGridSpec(
            num_scalar_prefetch=1,
            grid=(len(order),),
            in_specs=[whole] * 8 + [pl.BlockSpec((None, 2048, 256), lambda i, s: (placed(s)[5] ^ t, 0, 0))],
            out_specs=[whole] * len(order),
        ),
        name="second",
        compiler_params=pltpu.CompilerParams(vmem_limit_bytes=LIMIT),
        cost_estimate=pl.CostEstimate(
            flops=2 * 2 * ROWS * 2048 * 256 * len(order), bytes_accessed=(2 + len(order)) << 20, transcendentals=0
        ),
    )(idx, *left, w_all)[0]


def summed(parts, h, e, rows):
    total = parts[0][h, rows, lanes(e)].astype(F32)
    for part in parts[1:]:
        total += part[h, rows, lanes(e)].astype(F32)
    return total


def update_kernel(idx, *refs):
    parts, left, terms, nxt, outs = refs[:4], refs[4:8], refs[8:12], refs[-5], refs[-4:]
    d = placed(idx)[0]

    @pl.loop(0, 4)
    def _(i):
        rows = lanes(i)
        for j in range(4):
            h, e = (d ^ j) >> 1, (d ^ j) & 1
            ladder = summed(parts, h, e, rows)
            outs[j][rows] = ladder.astype(BF)
            step = terms[j][1, rows].astype(F32) * (terms[j][0, rows].astype(F32) + ladder)
            nxt[h, rows, lanes(e)] = (left[j][rows].astype(F32) - step).astype(BF)


def update(n, idx, parts, left, terms, carried):
    whole = pl.BlockSpec((2, ROWS, 256), lambda i, s: (0, 0, 0))
    quarter = pl.BlockSpec((ROWS, 128), lambda i, s: (n, 0))
    return pl.pallas_call(
        update_kernel,
        out_shape=[shape(2, ROWS, 256)] + [shape(512, 128)] * 4,
        grid_spec=pltpu.PrefetchScalarGridSpec(
            num_scalar_prefetch=1,
            grid=(1,),
            in_specs=[whole] * 4
            + [pl.BlockSpec((ROWS, 128), lambda i, s: (n, placed(s)[0]))] * 4
            + [pl.BlockSpec((2, ROWS, 128), lambda i, s: (0, n, 0))] * 4
            + [ANY] * len(carried),
            out_specs=[whole] + [quarter] * 4,
        ),
        compiler_params=pltpu.CompilerParams(vmem_limit_bytes=LIMIT),
        cost_estimate=pl.CostEstimate(flops=0, bytes_accessed=2 << 20, transcendentals=0),
        input_output_aliases={13 + i: 1 + i for i in range(len(carried))},
    )(idx, *parts, *left, *terms, *carried)


def sum_kernel(idx, *refs):
    parts, outs = refs[:-4], refs[-4:]
    d = placed(idx)[0]

    @pl.loop(0, 4)
    def _(i):
        rows = lanes(i)
        for j in range(4):
            outs[j][rows] = summed(parts, (d ^ j) >> 1, (d ^ j) & 1, rows).astype(BF)


def final_kernel(idx, amps, base, invd, *refs):
    first, second, new, res = refs[:4], refs[4:8], refs[-2], refs[-1]
    d = placed(idx)[0]

    @pl.loop(0, 4)
    def _(i):
        rows = lanes(i)
        for j in range(4):
            q = d ^ j
            keep = kept(idx, RMASK, i >> 1, q >> 1).astype(F32)
            fixed, inverse = base[rows, lanes(q)], invd[rows, lanes(q)]
            one = (fixed + first[j][rows].astype(F32)) * keep
            mid = (amps[rows, lanes(q)].astype(F32) - inverse * one).astype(BF).astype(F32)
            two = (fixed + second[j][rows].astype(F32)) * keep
            res[rows, lanes(q)] = two
            new[rows, lanes(q)] = (mid - inverse * two).astype(BF)


def compute(amps, ints, base, invd, am, im, rm):
    z, y = lax.axis_index("z"), lax.axis_index("y")
    xh, xl, c = lax.axis_index("xh"), lax.axis_index("xl"), lax.axis_index("c")
    place = (xh * 2 + xl) | (c << 2) | (z << 3) | (y << 6)
    idx = (am | (im << IMASK) | (rm << RMASK) | (place << 3)).astype(jnp.int32)

    cut = list(call(prep_w, [shape(512, 128)] * 4, [SM, VM], [VM] * 4)(idx, ints))
    for i in range(4):
        cut[i] = permute_x(cut[i], lambda h, l, k, i=i: (k ^ (i >> 1), l ^ (i & 1), h))
    own = [call(join_w, shape(1024, 128), [VM] * 2, VM)(cut[2 * a], cut[2 * a + 1]) for a in range(2)]

    masked = call(prep_a, shape(512, 512), [SM, VM], VM)(idx, amps)
    terms = call(prep_t, [shape(2, 512, 128)] * 4, [SM, VM, VM], [VM] * 4)(idx, base, invd)

    pieces = [[own[0]] + [None] * 7, [own[1]] + [None] * 7]
    up, down = list(own), list(own)
    for step in range(1, 4):
        for g in range(2):
            up[g] = shift_z(up[g], 1)
            down[g] = shift_z(down[g], -1)
            pieces[g][8 - step] = up[g]
            pieces[g][step] = down[g]
    pieces[0][4] = shift_z(up[0], 1)
    pieces[1][4] = shift_z(down[1], -1)

    left = [masked]
    for j in range(1, 4):
        left.append(chip_xor(masked, j))
    joined = call(join_a, shape(4, 512, 512), [VM] * 4, VM)(*left)
    left.append(core_swap(joined))
    terms = list(terms)
    for j in range(1, 4):
        terms[j] = chip_xor(terms[j], j)

    sends = first_product((0, 1), idx, pieces, left, [])
    sends = first_product((2,), idx, pieces, left, sends)
    sends = first_product((3,), idx, pieces, left, sends)
    w_all = call(arrange, shape(4, 2048, 256), [SM] + [VM] * 16, VM, moved=8 << 20)(idx, *pieces[0], *pieces[1])

    def reduced(sends):
        got = [sends[0]] + [None] * 3
        for t in (2, 1, 3):
            got[t] = xor_y(sends[t], t)
        return got

    def spread(values):
        got = [values[0]] + [None] * 3
        for j in (2, 1, 3):
            got[j] = chip_xor(values[j], j)
        return got

    nxt, *ladder = update(0, idx, reduced(sends), left[:4], terms, [])
    chips = spread([nxt] * 4)
    chips = chips + [core_swap(v) for v in chips]
    parts = [None] * 4
    for t in (2, 1, 3, 0):
        parts[t] = second_product(t, idx, chips, w_all)
    parts = reduced(parts)
    first = spread(ladder)
    ladder = call(sum_kernel, [shape(512, 128)] * 4, [SM] + [VM] * 4, [VM] * 4)(idx, *parts)
    second = spread(ladder)
    return call(
        final_kernel, [shape(512, 512), shape(512, 512, dtype=F32)], [SM] + [VM] * 11, [VM] * 2, moved=6 << 20
    )(idx, amps, base, invd, *first, *second)


def solution(mesh):
    split = Mesh(mesh.devices.reshape(8, 2, 4, 2, 2), ("z", "xh", "y", "xl", "c"))
    row, col = ("z", "xh"), ("y", "xl", "c")
    return jax.shard_map(
        compute,
        mesh=split,
        in_specs=(P(row, col), P(col, row), P(row, col), P(row, col), P(row, col), P(col, row), P(row, col)),
        out_specs=(P(row, col), P(row, col)),
        check_vma=False,
    )
```

profile of v0, /device:TPU:4, one launch (start us, length us, event | category | flops | bytes accessed | tf_op | source)
XLA Modules:
  0.0 200.1 jit_solution(16733197196290598758)
XLA Ops:
  6.6 11.3 %collective-permute-done.18.one.refs_17_.refs_9_.refs_5_ = bf16[512,512]{1,0:T(8,128)(2,1)S(1)} collective-permute-done((bf16[512,512]{1,0:T(8,128)(2,1)S(1)}, bf16[512,512]{1,0:T(8,128)(2,1)S(1)}, u32[]{:S(2)}, u32[]{:S(2)}) %collective-permute-start.18) | collective-permute-done | bytes 524320 | tf_op jit(solution)/shard_map/ppermute | solution.py:32
  17.9 10.2 %collective-permute-done.19.two.refs_18_.refs_10_.refs_6_ = bf16[512,512]{1,0:T(8,128)(2,1)S(1)} collective-permute-done((bf16[512,512]{1,0:T(8,128)(2,1)S(1)}, bf16[512,512]{1,0:T(8,128)(2,1)S(1)}, u32[]{:S(2)}, u32[]{:S(2)}) %collective-permute-start.19) | collective-permute-done | bytes 524320 | tf_op jit(solution)/shard_map/ppermute | solution.py:32
  30.4 5.9 %collective-permute-start = (bf16[512,128]{1,0:T(8,128)(2,1)S(1)}, bf16[512,128]{1,0:T(8,128)(2,1)S(1)}, u32[]{:S(2)}, u32[]{:S(2)}) collective-permute-start(bf16[512,128]{1,0:T(8,128)(2,1)S(1)} %get-tuple-element.31), channel_id=1, source_target_pairs={{0,0},{1,16},{2,2},{3,18},{16,1},{17,17},{18,3},{19,19},{4,4},{5,2... | collective-permute-start | bytes 393224 | tf_op jit(solution)/shard_map/ppermute | solution.py:32
  36.5 3.4 %collective-permute-start.7 = (bf16[512,128]{1,0:T(8,128)(2,1)S(1)}, bf16[512,128]{1,0:T(8,128)(2,1)S(1)}, u32[]{:S(2)}, u32[]{:S(2)}) collective-permute-start(bf16[512,128]{1,0:T(8,128)(2,1)S(1)} %get-tuple-element.34), channel_id=1, source_target_pairs={{0,18},{1,2},{2,16},{3,0},{16,19},{17,3},{18,17},{19,1},{4,22},{5,... | collective-permute-start | bytes 393224 | tf_op jit(solution)/shard_map/ppermute | solution.py:32
  44.3 5.9 %collective-permute-start.8 = (bf16[1024,128]{1,0:T(8,128)(2,1)S(1)}, bf16[1024,128]{1,0:T(8,128)(2,1)S(1)}, u32[]{:S(2)}, u32[]{:S(2)}) collective-permute-start(bf16[1024,128]{1,0:T(8,128)(2,1)S(1)} %shard_map.88.refs_1_.refs_7_.refs_8_), channel_id=1, source_target_pairs={{0,224},{32,0},{64,32},{96,64},{128,96},{160,128},{192,160},{224,1... | collective-permute-start | bytes 786440 | tf_op jit(solution)/shard_map/ppermute | solution.py:44
  50.2 3.2 %collective-permute-start.15 = (bf16[1024,128]{1,0:T(8,128)(2,1)S(1)}, bf16[1024,128]{1,0:T(8,128)(2,1)S(1)}, u32[]{:S(2)}, u32[]{:S(2)}) collective-permute-start(bf16[1024,128]{1,0:T(8,128)(2,1)S(1)} %shard_map.87.refs_0_.refs_6_), channel_id=1, source_target_pairs={{0,224},{32,0},{64,32},{96,64},{128,96},{160,128},{192,160},{224,1... | collective-permute-start | bytes 786440 | tf_op jit(solution)/shard_map/ppermute | solution.py:44
  53.5 3.5 %collective-permute-done.8.refs_3_.refs_13_.refs_9_ = bf16[1024,128]{1,0:T(8,128)(2,1)S(1)} collective-permute-done((bf16[1024,128]{1,0:T(8,128)(2,1)S(1)}, bf16[1024,128]{1,0:T(8,128)(2,1)S(1)}, u32[]{:S(2)}, u32[]{:S(2)}) %collective-permute-start.8) | collective-permute-done | bytes 262176 | tf_op jit(solution)/shard_map/ppermute | solution.py:44
  56.9 3.7 %collective-permute-start.9 = (bf16[1024,128]{1,0:T(8,128)(2,1)S(1)}, bf16[1024,128]{1,0:T(8,128)(2,1)S(1)}, u32[]{:S(2)}, u32[]{:S(2)}) collective-permute-start(bf16[1024,128]{1,0:T(8,128)(2,1)S(1)} %collective-permute-done.8.refs_3_.refs_13_.refs_9_), channel_id=1, source_target_pairs={{0,224},{32,0},{64,32},{96,64},{128,96},{160,128},{192,160},{224,1... | collective-permute-start | bytes 786440 | tf_op jit(solution)/shard_map/ppermute | solution.py:44
  62.5 3.7 %collective-permute-start.16 = (bf16[1024,128]{1,0:T(8,128)(2,1)S(1)}, bf16[1024,128]{1,0:T(8,128)(2,1)S(1)}, u32[]{:S(2)}, u32[]{:S(2)}) collective-permute-start(bf16[1024,128]{1,0:T(8,128)(2,1)S(1)} %collective-permute-done.15.refs_2_.refs_12_.refs_1_), channel_id=1, source_target_pairs={{0,224},{32,0},{64,32},{96,64},{128,96},{160,128},{192,160},{224,1... | collective-permute-start | bytes 786440 | tf_op jit(solution)/shard_map/ppermute | solution.py:44
  68.2 3.7 %collective-permute-start.10 = (bf16[1024,128]{1,0:T(8,128)(2,1)S(1)}, bf16[1024,128]{1,0:T(8,128)(2,1)S(1)}, u32[]{:S(2)}, u32[]{:S(2)}) collective-permute-start(bf16[1024,128]{1,0:T(8,128)(2,1)S(1)} %collective-permute-done.9.refs_15_.refs_1_.refs_10_), channel_id=1, source_target_pairs={{0,224},{32,0},{64,32},{96,64},{128,96},{160,128},{192,160},{224,1... | collective-permute-start | bytes 786440 | tf_op jit(solution)/shard_map/ppermute | solution.py:44
  73.8 3.7 %collective-permute-start.17 = (bf16[1024,128]{1,0:T(8,128)(2,1)S(1)}, bf16[1024,128]{1,0:T(8,128)(2,1)S(1)}, u32[]{:S(2)}, u32[]{:S(2)}) collective-permute-start(bf16[1024,128]{1,0:T(8,128)(2,1)S(1)} %collective-permute-done.16.refs_14_.refs_0_.refs_2_), channel_id=1, source_target_pairs={{0,224},{32,0},{64,32},{96,64},{128,96},{160,128},{192,160},{224,1... | collective-permute-start | bytes 786440 | tf_op jit(solution)/shard_map/ppermute | solution.py:44
  79.6 3.5 %collective-permute-start.11 = (bf16[1024,128]{1,0:T(8,128)(2,1)S(1)}, bf16[1024,128]{1,0:T(8,128)(2,1)S(1)}, u32[]{:S(2)}, u32[]{:S(2)}) collective-permute-start(bf16[1024,128]{1,0:T(8,128)(2,1)S(1)} %collective-permute-done.10.refs_3_.refs_5_.refs_11_), channel_id=1, source_target_pairs={{0,224},{32,0},{64,32},{96,64},{128,96},{160,128},{192,160},{224,1... | collective-permute-start | bytes 786440 | tf_op jit(solution)/shard_map/ppermute | solution.py:44
  83.1 3.6 %shard_map.91 = (bf16[2,512,256]{2,1,0:T(8,128)(2,1)S(1)}, bf16[2,512,256]{2,1,0:T(8,128)(2,1)S(1)}, bf16[2,512,256]{2,1,0:T(8,128)(2,1)S(1)}, bf16[2,512,256]{2,1,0:T(8,128)(2,1)S(1)}) custom-call(s32[2,2]{1,0:T(2,128)S(1)} %or_or_fusion.idx, bf16[1024,128]{1,0:T(8,128)(2,1)S(1)} %shard_map.87.refs_0_.refs_6_, ...), custom_call_target="tpu_custom_call" | custom-call | flops 2147483648 | bytes 2097152 | tf_op jit(solution)/shard_map/pallas_call | solution.py:163
  86.7 2.1 %shard_map.92 = (bf16[2,512,256]{2,1,0:T(8,128)(2,1)S(1)}, bf16[2,512,256]{2,1,0:T(8,128)(2,1)S(1)}, bf16[2,512,256]{2,1,0:T(8,128)(2,1)S(1)}, bf16[2,512,256]{2,1,0:T(8,128)(2,1)S(1)}) custom-call(s32[2,2]{1,0:T(2,128)S(1)} %or_or_fusion.idx, ...), custom_call_target="tpu_custom_call", output_to_operand_aliasing={{0}: (14, {}), {1}: (15, {}), {2}: (16, {}), {3}: (17, {})} | custom-call | flops 1073741824 | bytes 1048576 | tf_op jit(solution)/shard_map/pallas_call | solution.py:163
  89.3 2.1 %shard_map.93 = (bf16[2,512,256]{2,1,0:T(8,128)(2,1)S(1)}, bf16[2,512,256]{2,1,0:T(8,128)(2,1)S(1)}, bf16[2,512,256]{2,1,0:T(8,128)(2,1)S(1)}, bf16[2,512,256]{2,1,0:T(8,128)(2,1)S(1)}) custom-call(s32[2,2]{1,0:T(2,128)S(1)} %or_or_fusion.idx, ...), custom_call_target="tpu_custom_call", output_to_operand_aliasing={{0}: (14, {}), {1}: (15, {}), {2}: (16, {}), {3}: (17, {})} | custom-call | flops 1073741824 | bytes 1048576 | tf_op jit(solution)/shard_map/pallas_call | solution.py:163
  93.0 2.9 %collective-permute-start.23 = (bf16[2,512,256]{2,1,0:T(8,128)(2,1)S(1)}, bf16[2,512,256]{2,1,0:T(8,128)(2,1)S(1)}, u32[]{:S(2)}, u32[]{:S(2)}) collective-permute-start(bf16[2,512,256]{2,1,0:T(8,128)(2,1)S(1)} %get-tuple-element.45), channel_id=1, source_target_pairs={{0,8},{4,12},{8,0},{12,4},{1,9},{5,13},{9,1},{13,5},{2,10},{6,14},... | collective-permute-start | bytes 1572872 | tf_op jit(solution)/shard_map/ppermute | solution.py:48
  98.7 5.3 %collective-permute-done.26.refs_10_ = bf16[2,512,128]{2,1,0:T(8,128)(2,1)S(1)} collective-permute-done((bf16[2,512,128]{2,1,0:T(8,128)(2,1)S(1)}, bf16[2,512,128]{2,1,0:T(8,128)(2,1)S(1)}, u32[]{:S(2)}, u32[]{:S(2)}) %collective-permute-start.26) | collective-permute-done | bytes 262176 | tf_op jit(solution)/shard_map/ppermute | solution.py:32
  104.0 5.5 %collective-permute-done.27.refs_11_ = bf16[2,512,128]{2,1,0:T(8,128)(2,1)S(1)} collective-permute-done((bf16[2,512,128]{2,1,0:T(8,128)(2,1)S(1)}, bf16[2,512,128]{2,1,0:T(8,128)(2,1)S(1)}, u32[]{:S(2)}, u32[]{:S(2)}) %collective-permute-start.27) | collective-permute-done | bytes 262176 | tf_op jit(solution)/shard_map/ppermute | solution.py:32
  109.5 8.4 %collective-permute-done.23.refs_2_ = bf16[2,512,256]{2,1,0:T(8,128)(2,1)S(1)} collective-permute-done((bf16[2,512,256]{2,1,0:T(8,128)(2,1)S(1)}, bf16[2,512,256]{2,1,0:T(8,128)(2,1)S(1)}, u32[]{:S(2)}, u32[]{:S(2)}) %collective-permute-start.23) | collective-permute-done | bytes 524320 | tf_op jit(solution)/shard_map/ppermute | solution.py:48
  117.9 2.6 %collective-permute-done.24.refs_3_ = bf16[2,512,256]{2,1,0:T(8,128)(2,1)S(1)} collective-permute-done((bf16[2,512,256]{2,1,0:T(8,128)(2,1)S(1)}, bf16[2,512,256]{2,1,0:T(8,128)(2,1)S(1)}, u32[]{:S(2)}, u32[]{:S(2)}) %collective-permute-start.24) | collective-permute-done | bytes 524320 | tf_op jit(solution)/shard_map/ppermute | solution.py:48
  123.0 2.5 %collective-permute-start.32 = (bf16[2,512,256]{2,1,0:T(8,128)(2,1)S(1)}, bf16[2,512,256]{2,1,0:T(8,128)(2,1)S(1)}, u32[]{:S(2)}, u32[]{:S(2)}) collective-permute-start(bf16[2,512,256]{2,1,0:T(8,128)(2,1)S(1)} %get-tuple-element.55.refs_0_), channel_id=1, source_target_pairs={{0,16},{1,17},{2,18},{3,19},{16,0},{17,1},{18,2},{19,3},{4,20},{5,... | collective-permute-start | bytes 1572872 | tf_op jit(solution)/shard_map/ppermute | solution.py:32
  125.8 8.9 %collective-permute-done.31.refs_1_ = bf16[2,512,256]{2,1,0:T(8,128)(2,1)S(1)} collective-permute-done((bf16[2,512,256]{2,1,0:T(8,128)(2,1)S(1)}, bf16[2,512,256]{2,1,0:T(8,128)(2,1)S(1)}, u32[]{:S(2)}, u32[]{:S(2)}) %collective-permute-start.31) | collective-permute-done | bytes 524320 | tf_op jit(solution)/shard_map/ppermute | solution.py:32
  134.7 13.4 %collective-permute-done.32.refs_2_ = bf16[2,512,256]{2,1,0:T(8,128)(2,1)S(1)} collective-permute-done((bf16[2,512,256]{2,1,0:T(8,128)(2,1)S(1)}, bf16[2,512,256]{2,1,0:T(8,128)(2,1)S(1)}, u32[]{:S(2)}, u32[]{:S(2)}) %collective-permute-start.32) | collective-permute-done | bytes 524320 | tf_op jit(solution)/shard_map/ppermute | solution.py:32
  149.6 2.3 %shard_map.96.refs_8_ = bf16[4,2048,256]{2,1,0:T(8,128)(2,1)S(1)} custom-call(s32[2,2]{1,0:T(2,128)S(1)} %or_or_fusion.idx, bf16[1024,128]{1,0:T(8,128)(2,1)S(1)} %shard_map.87.refs_0_.refs_6_, bf16[1024,128]{1,0:T(8,128)(2,1)S(1)} %collective-permute-done.15.refs_2_.refs_12_.refs_1_, bf16[1024,128]{1,0:T(8,128)(2,1)S(1)} %collective-permute-done.16.refs_14_.refs_0_.refs_2_, ...), custom_call_target="tpu_custom_call" | custom-call | bytes 8388608 | tf_op jit(solution)/shard_map/pallas_call | solution.py:338
  159.8 3.0 %collective-permute-start.40 = (bf16[2,512,256]{2,1,0:T(8,128)(2,1)S(1)}, bf16[2,512,256]{2,1,0:T(8,128)(2,1)S(1)}, u32[]{:S(2)}, u32[]{:S(2)}) collective-permute-start(bf16[2,512,256]{2,1,0:T(8,128)(2,1)S(1)} %second.7), channel_id=1, source_target_pairs={{0,12},{4,8},{8,4},{12,0},{1,13},{5,9},{9,5},{13,1},{2,14},{6,10},... | collective-permute-start | bytes 1572872 | tf_op jit(solution)/shard_map/ppermute | solution.py:48
  162.8 3.5 %collective-permute-start.28 = (bf16[512,128]{1,0:T(8,128)(2,1)S(1)}, bf16[512,128]{1,0:T(8,128)(2,1)S(1)}, u32[]{:S(2)}, u32[]{:S(2)}) collective-permute-start(bf16[512,128]{1,0:T(8,128)(2,1)S(1)} %get-tuple-element.52), channel_id=1, source_target_pairs={{0,2},{1,3},{2,0},{3,1},{16,18},{17,19},{18,16},{19,17},{4,6},{5,7... | collective-permute-start | bytes 393224 | tf_op jit(solution)/shard_map/ppermute | solution.py:32
  169.8 9.6 %collective-permute-done.39.refs_2_ = bf16[2,512,256]{2,1,0:T(8,128)(2,1)S(1)} collective-permute-done((bf16[2,512,256]{2,1,0:T(8,128)(2,1)S(1)}, bf16[2,512,256]{2,1,0:T(8,128)(2,1)S(1)}, u32[]{:S(2)}, u32[]{:S(2)}) %collective-permute-start.39) | collective-permute-done | bytes 524320 | tf_op jit(solution)/shard_map/ppermute | solution.py:48
  179.4 6.7 %collective-permute-done.40.refs_3_ = bf16[2,512,256]{2,1,0:T(8,128)(2,1)S(1)} collective-permute-done((bf16[2,512,256]{2,1,0:T(8,128)(2,1)S(1)}, bf16[2,512,256]{2,1,0:T(8,128)(2,1)S(1)}, u32[]{:S(2)}, u32[]{:S(2)}) %collective-permute-start.40) | collective-permute-done | bytes 524320 | tf_op jit(solution)/shard_map/ppermute | solution.py:48
  187.0 3.5 %collective-permute-start.41 = (bf16[512,128]{1,0:T(8,128)(2,1)S(1)}, bf16[512,128]{1,0:T(8,128)(2,1)S(1)}, u32[]{:S(2)}, u32[]{:S(2)}) collective-permute-start(bf16[512,128]{1,0:T(8,128)(2,1)S(1)} %get-tuple-element.57), channel_id=1, source_target_pairs={{0,2},{1,3},{2,0},{3,1},{16,18},{17,19},{18,16},{19,17},{4,6},{5,7... | collective-permute-start | bytes 393224 | tf_op jit(solution)/shard_map/ppermute | solution.py:32
  192.1 2.6 %collective-permute-done.41.refs_5_ = bf16[512,128]{1,0:T(8,128)(2,1)S(1)} collective-permute-done((bf16[512,128]{1,0:T(8,128)(2,1)S(1)}, bf16[512,128]{1,0:T(8,128)(2,1)S(1)}, u32[]{:S(2)}, u32[]{:S(2)}) %collective-permute-start.41) | collective-permute-done | bytes 131104 | tf_op jit(solution)/shard_map/ppermute | solution.py:32
  194.7 2.4 %collective-permute-done.42.refs_6_ = bf16[512,128]{1,0:T(8,128)(2,1)S(1)} collective-permute-done((bf16[512,128]{1,0:T(8,128)(2,1)S(1)}, bf16[512,128]{1,0:T(8,128)(2,1)S(1)}, u32[]{:S(2)}, u32[]{:S(2)}) %collective-permute-start.42) | collective-permute-done | bytes 131104 | tf_op jit(solution)/shard_map/ppermute | solution.py:32
  197.7 2.4 %shard_map.98 = (bf16[512,512]{1,0:T(8,128)(2,1)}, f32[512,512]{1,0:T(8,128)}) custom-call(s32[2,2]{1,0:T(2,128)S(1)} %or_or_fusion.idx, bf16[512,512]{1,0:T(8,128)(2,1)S(1)} %copy-done.3, f32[512,512]{1,0:T(8,128)S(1)} %copy-done, f32[512,512]{1,0:T(8,128)S(1)} %copy-done.1, bf16[512,128]{1,0:T(8,128)(2,1)S(1)} %get-tuple-element.51.refs_0_, ...), custom_call_target="tpu_custom_call" | custom-call | bytes 6291456 | tf_op jit(solution)/shard_map/pallas_call | solution.py:362
  (84 shorter events, 44.2 us)
Async XLA Ops:
  3.0 14.9 %collective-permute-start.18 = (bf16[512,512]{1,0:T(8,128)(2,1)S(1)}, bf16[512,512]{1,0:T(8,128)(2,1)S(1)}, u32[]{:S(2)}, u32[]{:S(2)}) collective-permute-start(bf16[512,512]{1,0:T(8,128)(2,1)S(1)} %shard_map.89.zero.refs_16_.refs_8_.refs_4_), channel_id=1, source_target_pairs={{0,2},{1,3},{2,0},{3,1},{16,18},{17,19},{18,16},{19,17},{4,6},{5,7... | collective-permute-start | bytes 1572872 | tf_op jit(solution)/shard_map/ppermute | solution.py:32
  4.3 23.8 %collective-permute-start.19 = (bf16[512,512]{1,0:T(8,128)(2,1)S(1)}, bf16[512,512]{1,0:T(8,128)(2,1)S(1)}, u32[]{:S(2)}, u32[]{:S(2)}) collective-permute-start(bf16[512,512]{1,0:T(8,128)(2,1)S(1)} %shard_map.89.zero.refs_16_.refs_8_.refs_4_), channel_id=1, source_target_pairs={{0,16},{1,17},{2,18},{3,19},{16,0},{17,1},{18,2},{19,3},{4,20},{5,... | collective-permute-start | bytes 1572872 | tf_op jit(solution)/shard_map/ppermute | solution.py:32
  5.4 24.0 %collective-permute-start.20 = (bf16[512,512]{1,0:T(8,128)(2,1)S(1)}, bf16[512,512]{1,0:T(8,128)(2,1)S(1)}, u32[]{:S(2)}, u32[]{:S(2)}) collective-permute-start(bf16[512,512]{1,0:T(8,128)(2,1)S(1)} %shard_map.89.zero.refs_16_.refs_8_.refs_4_), channel_id=1, source_target_pairs={{0,18},{1,19},{2,16},{3,17},{16,2},{17,3},{18,0},{19,1},{4,22},{5,... | collective-permute-start | bytes 1572872 | tf_op jit(solution)/shard_map/ppermute | solution.py:32
  29.6 50.0 %collective-permute-start.21 = (bf16[4,512,512]{2,1,0:T(8,128)(2,1)S(1)}, bf16[4,512,512]{2,1,0:T(8,128)(2,1)S(1)}, u32[]{:S(2)}, u32[]{:S(2)}) collective-permute-start(bf16[4,512,512]{2,1,0:T(8,128)(2,1)S(1)} %shard_map.90), channel_id=1, source_target_pairs={{0,1},{1,0},{2,3},{3,2},{16,17},{17,16},{18,19},{19,18},{4,5},{5,4... | collective-permute-start | bytes 6291464 | tf_op jit(solution)/shard_map/ppermute | solution.py:32
  41.1 12.4 %collective-permute-start.2 = (bf16[1024,128]{1,0:T(8,128)(2,1)S(1)}, bf16[1024,128]{1,0:T(8,128)(2,1)S(1)}, u32[]{:S(2)}, u32[]{:S(2)}) collective-permute-start(bf16[1024,128]{1,0:T(8,128)(2,1)S(1)} %shard_map.87.refs_0_.refs_6_), channel_id=1, source_target_pairs={{0,32},{32,64},{64,96},{96,128},{128,160},{160,192},{192,224},{224... | collective-permute-start | bytes 786440 | tf_op jit(solution)/shard_map/ppermute | solution.py:44
  44.3 12.6 %collective-permute-start.8 = (bf16[1024,128]{1,0:T(8,128)(2,1)S(1)}, bf16[1024,128]{1,0:T(8,128)(2,1)S(1)}, u32[]{:S(2)}, u32[]{:S(2)}) collective-permute-start(bf16[1024,128]{1,0:T(8,128)(2,1)S(1)} %shard_map.88.refs_1_.refs_7_.refs_8_), channel_id=1, source_target_pairs={{0,224},{32,0},{64,32},{96,64},{128,96},{160,128},{192,160},{224,1... | collective-permute-start | bytes 786440 | tf_op jit(solution)/shard_map/ppermute | solution.py:44
  50.2 10.4 %collective-permute-start.12 = (bf16[1024,128]{1,0:T(8,128)(2,1)S(1)}, bf16[1024,128]{1,0:T(8,128)(2,1)S(1)}, u32[]{:S(2)}, u32[]{:S(2)}) collective-permute-start(bf16[1024,128]{1,0:T(8,128)(2,1)S(1)} %shard_map.88.refs_1_.refs_7_.refs_8_), channel_id=1, source_target_pairs={{0,32},{32,64},{64,96},{96,128},{128,160},{160,192},{192,224},{224... | collective-permute-start | bytes 786440 | tf_op jit(solution)/shard_map/ppermute | solution.py:44
  50.2 12.3 %collective-permute-start.15 = (bf16[1024,128]{1,0:T(8,128)(2,1)S(1)}, bf16[1024,128]{1,0:T(8,128)(2,1)S(1)}, u32[]{:S(2)}, u32[]{:S(2)}) collective-permute-start(bf16[1024,128]{1,0:T(8,128)(2,1)S(1)} %shard_map.87.refs_0_.refs_6_), channel_id=1, source_target_pairs={{0,224},{32,0},{64,32},{96,64},{128,96},{160,128},{192,160},{224,1... | collective-permute-start | bytes 786440 | tf_op jit(solution)/shard_map/ppermute | solution.py:44
  53.5 12.8 %collective-permute-start.3 = (bf16[1024,128]{1,0:T(8,128)(2,1)S(1)}, bf16[1024,128]{1,0:T(8,128)(2,1)S(1)}, u32[]{:S(2)}, u32[]{:S(2)}) collective-permute-start(bf16[1024,128]{1,0:T(8,128)(2,1)S(1)} %collective-permute-done.2.refs_4_.refs_10_.refs_7_), channel_id=1, source_target_pairs={{0,32},{32,64},{64,96},{96,128},{128,160},{160,192},{192,224},{224... | collective-permute-start | bytes 786440 | tf_op jit(solution)/shard_map/ppermute | solution.py:44
  56.9 11.2 %collective-permute-start.9 = (bf16[1024,128]{1,0:T(8,128)(2,1)S(1)}, bf16[1024,128]{1,0:T(8,128)(2,1)S(1)}, u32[]{:S(2)}, u32[]{:S(2)}) collective-permute-start(bf16[1024,128]{1,0:T(8,128)(2,1)S(1)} %collective-permute-done.8.refs_3_.refs_13_.refs_9_), channel_id=1, source_target_pairs={{0,224},{32,0},{64,32},{96,64},{128,96},{160,128},{192,160},{224,1... | collective-permute-start | bytes 786440 | tf_op jit(solution)/shard_map/ppermute | solution.py:44
  60.6 11.2 %collective-permute-start.13 = (bf16[1024,128]{1,0:T(8,128)(2,1)S(1)}, bf16[1024,128]{1,0:T(8,128)(2,1)S(1)}, u32[]{:S(2)}, u32[]{:S(2)}) collective-permute-start(bf16[1024,128]{1,0:T(8,128)(2,1)S(1)} %collective-permute-done.12.refs_5_.refs_11_.refs_15_), channel_id=1, source_target_pairs={{0,32},{32,64},{64,96},{96,128},{128,160},{160,192},{192,224},{224... | collective-permute-start | bytes 786440 | tf_op jit(solution)/shard_map/ppermute | solution.py:44
  62.5 11.2 %collective-permute-start.16 = (bf16[1024,128]{1,0:T(8,128)(2,1)S(1)}, bf16[1024,128]{1,0:T(8,128)(2,1)S(1)}, u32[]{:S(2)}, u32[]{:S(2)}) collective-permute-start(bf16[1024,128]{1,0:T(8,128)(2,1)S(1)} %collective-permute-done.15.refs_2_.refs_12_.refs_1_), channel_id=1, source_target_pairs={{0,224},{32,0},{64,32},{96,64},{128,96},{160,128},{192,160},{224,1... | collective-permute-start | bytes 786440 | tf_op jit(solution)/shard_map/ppermute | solution.py:44
  66.2 12.1 %collective-permute-start.4 = (bf16[1024,128]{1,0:T(8,128)(2,1)S(1)}, bf16[1024,128]{1,0:T(8,128)(2,1)S(1)}, u32[]{:S(2)}, u32[]{:S(2)}) collective-permute-start(bf16[1024,128]{1,0:T(8,128)(2,1)S(1)} %collective-permute-done.3.refs_8_.refs_6_), channel_id=1, source_target_pairs={{0,32},{32,64},{64,96},{96,128},{128,160},{160,192},{192,224},{224... | collective-permute-start | bytes 786440 | tf_op jit(solution)/shard_map/ppermute | solution.py:44
  68.2 11.4 %collective-permute-start.10 = (bf16[1024,128]{1,0:T(8,128)(2,1)S(1)}, bf16[1024,128]{1,0:T(8,128)(2,1)S(1)}, u32[]{:S(2)}, u32[]{:S(2)}) collective-permute-start(bf16[1024,128]{1,0:T(8,128)(2,1)S(1)} %collective-permute-done.9.refs_15_.refs_1_.refs_10_), channel_id=1, source_target_pairs={{0,224},{32,0},{64,32},{96,64},{128,96},{160,128},{192,160},{224,1... | collective-permute-start | bytes 786440 | tf_op jit(solution)/shard_map/ppermute | solution.py:44
  71.9 14.8 %collective-permute-start.14 = (bf16[1024,128]{1,0:T(8,128)(2,1)S(1)}, bf16[1024,128]{1,0:T(8,128)(2,1)S(1)}, u32[]{:S(2)}, u32[]{:S(2)}) collective-permute-start(bf16[1024,128]{1,0:T(8,128)(2,1)S(1)} %collective-permute-done.13.refs_9_.refs_7_.refs_14_), channel_id=1, source_target_pairs={{0,32},{32,64},{64,96},{96,128},{128,160},{160,192},{192,224},{224... | collective-permute-start | bytes 786440 | tf_op jit(solution)/shard_map/ppermute | solution.py:44
  73.8 12.9 %collective-permute-start.17 = (bf16[1024,128]{1,0:T(8,128)(2,1)S(1)}, bf16[1024,128]{1,0:T(8,128)(2,1)S(1)}, u32[]{:S(2)}, u32[]{:S(2)}) collective-permute-start(bf16[1024,128]{1,0:T(8,128)(2,1)S(1)} %collective-permute-done.16.refs_14_.refs_0_.refs_2_), channel_id=1, source_target_pairs={{0,224},{32,0},{64,32},{96,64},{128,96},{160,128},{192,160},{224,1... | collective-permute-start | bytes 786440 | tf_op jit(solution)/shard_map/ppermute | solution.py:44
  78.3 19.0 %collective-permute-start.25 = (bf16[2,512,128]{2,1,0:T(8,128)(2,1)S(1)}, bf16[2,512,128]{2,1,0:T(8,128)(2,1)S(1)}, u32[]{:S(2)}, u32[]{:S(2)}) collective-permute-start(bf16[2,512,128]{2,1,0:T(8,128)(2,1)S(1)} %get-tuple-element.48), channel_id=1, source_target_pairs={{0,2},{1,3},{2,0},{3,1},{16,18},{17,19},{18,16},{19,17},{4,6},{5,7... | collective-permute-start | bytes 786440 | tf_op jit(solution)/shard_map/ppermute | solution.py:32
  91.4 18.1 %collective-permute-start.22 = (bf16[2,512,256]{2,1,0:T(8,128)(2,1)S(1)}, bf16[2,512,256]{2,1,0:T(8,128)(2,1)S(1)}, u32[]{:S(2)}, u32[]{:S(2)}) collective-permute-start(bf16[2,512,256]{2,1,0:T(8,128)(2,1)S(1)} %get-tuple-element.44), channel_id=1, source_target_pairs={{0,4},{4,0},{8,12},{12,8},{1,5},{5,1},{9,13},{13,9},{2,6},{6,2},{1... | collective-permute-start | bytes 1572872 | tf_op jit(solution)/shard_map/ppermute | solution.py:48
  93.0 24.8 %collective-permute-start.23 = (bf16[2,512,256]{2,1,0:T(8,128)(2,1)S(1)}, bf16[2,512,256]{2,1,0:T(8,128)(2,1)S(1)}, u32[]{:S(2)}, u32[]{:S(2)}) collective-permute-start(bf16[2,512,256]{2,1,0:T(8,128)(2,1)S(1)} %get-tuple-element.45), channel_id=1, source_target_pairs={{0,8},{4,12},{8,0},{12,4},{1,9},{5,13},{9,1},{13,5},{2,10},{6,14},... | collective-permute-start | bytes 1572872 | tf_op jit(solution)/shard_map/ppermute | solution.py:48
  95.9 24.5 %collective-permute-start.24 = (bf16[2,512,256]{2,1,0:T(8,128)(2,1)S(1)}, bf16[2,512,256]{2,1,0:T(8,128)(2,1)S(1)}, u32[]{:S(2)}, u32[]{:S(2)}) collective-permute-start(bf16[2,512,256]{2,1,0:T(8,128)(2,1)S(1)} %get-tuple-element.46), channel_id=1, source_target_pairs={{0,12},{4,8},{8,4},{12,0},{1,13},{5,9},{9,5},{13,1},{2,14},{6,10},... | collective-permute-start | bytes 1572872 | tf_op jit(solution)/shard_map/ppermute | solution.py:48
  97.3 12.2 %collective-permute-start.27 = (bf16[2,512,128]{2,1,0:T(8,128)(2,1)S(1)}, bf16[2,512,128]{2,1,0:T(8,128)(2,1)S(1)}, u32[]{:S(2)}, u32[]{:S(2)}) collective-permute-start(bf16[2,512,128]{2,1,0:T(8,128)(2,1)S(1)} %get-tuple-element.50), channel_id=1, source_target_pairs={{0,18},{1,19},{2,16},{3,17},{16,2},{17,3},{18,0},{19,1},{4,22},{5,... | collective-permute-start | bytes 786440 | tf_op jit(solution)/shard_map/ppermute | solution.py:32
  121.6 13.0 %collective-permute-start.31 = (bf16[2,512,256]{2,1,0:T(8,128)(2,1)S(1)}, bf16[2,512,256]{2,1,0:T(8,128)(2,1)S(1)}, u32[]{:S(2)}, u32[]{:S(2)}) collective-permute-start(bf16[2,512,256]{2,1,0:T(8,128)(2,1)S(1)} %get-tuple-element.55.refs_0_), channel_id=1, source_target_pairs={{0,2},{1,3},{2,0},{3,1},{16,18},{17,19},{18,16},{19,17},{4,6},{5,7... | collective-permute-start | bytes 1572872 | tf_op jit(solution)/shard_map/ppermute | solution.py:32
  123.0 25.1 %collective-permute-start.32 = (bf16[2,512,256]{2,1,0:T(8,128)(2,1)S(1)}, bf16[2,512,256]{2,1,0:T(8,128)(2,1)S(1)}, u32[]{:S(2)}, u32[]{:S(2)}) collective-permute-start(bf16[2,512,256]{2,1,0:T(8,128)(2,1)S(1)} %get-tuple-element.55.refs_0_), channel_id=1, source_target_pairs={{0,16},{1,17},{2,18},{3,19},{16,0},{17,1},{18,2},{19,3},{4,20},{5,... | collective-permute-start | bytes 1572872 | tf_op jit(solution)/shard_map/ppermute | solution.py:32
  125.5 24.1 %collective-permute-start.33 = (bf16[2,512,256]{2,1,0:T(8,128)(2,1)S(1)}, bf16[2,512,256]{2,1,0:T(8,128)(2,1)S(1)}, u32[]{:S(2)}, u32[]{:S(2)}) collective-permute-start(bf16[2,512,256]{2,1,0:T(8,128)(2,1)S(1)} %get-tuple-element.55.refs_0_), channel_id=1, source_target_pairs={{0,18},{1,19},{2,16},{3,17},{16,2},{17,3},{18,0},{19,1},{4,22},{5,... | collective-permute-start | bytes 1572872 | tf_op jit(solution)/shard_map/ppermute | solution.py:32
  125.7 26.1 %collective-permute-start.34 = (bf16[2,512,256]{2,1,0:T(8,128)(2,1)S(1)}, bf16[2,512,256]{2,1,0:T(8,128)(2,1)S(1)}, u32[]{:S(2)}, u32[]{:S(2)}) collective-permute-start(bf16[2,512,256]{2,1,0:T(8,128)(2,1)S(1)} %get-tuple-element.55.refs_0_), channel_id=1, source_target_pairs={{0,1},{1,0},{2,3},{3,2},{16,17},{17,16},{18,19},{19,18},{4,5},{5,4... | collective-permute-start | bytes 1572872 | tf_op jit(solution)/shard_map/ppermute | solution.py:32
  134.7 17.2 %collective-permute-start.35 = (bf16[2,512,256]{2,1,0:T(8,128)(2,1)S(1)}, bf16[2,512,256]{2,1,0:T(8,128)(2,1)S(1)}, u32[]{:S(2)}, u32[]{:S(2)}) collective-permute-start(bf16[2,512,256]{2,1,0:T(8,128)(2,1)S(1)} %collective-permute-done.31.refs_1_), channel_id=1, source_target_pairs={{0,1},{1,0},{2,3},{3,2},{16,17},{17,16},{18,19},{19,18},{4,5},{5,4... | collective-permute-start | bytes 1572872 | tf_op jit(solution)/shard_map/ppermute | solution.py:32
  153.9 14.9 %collective-permute-start.38 = (bf16[2,512,256]{2,1,0:T(8,128)(2,1)S(1)}, bf16[2,512,256]{2,1,0:T(8,128)(2,1)S(1)}, u32[]{:S(2)}, u32[]{:S(2)}) collective-permute-start(bf16[2,512,256]{2,1,0:T(8,128)(2,1)S(1)} %second.5), channel_id=1, source_target_pairs={{0,4},{4,0},{8,12},{12,8},{1,5},{5,1},{9,13},{13,9},{2,6},{6,2},{1... | collective-permute-start | bytes 1572872 | tf_op jit(solution)/shard_map/ppermute | solution.py:48
  156.0 23.5 %collective-permute-start.39 = (bf16[2,512,256]{2,1,0:T(8,128)(2,1)S(1)}, bf16[2,512,256]{2,1,0:T(8,128)(2,1)S(1)}, u32[]{:S(2)}, u32[]{:S(2)}) collective-permute-start(bf16[2,512,256]{2,1,0:T(8,128)(2,1)S(1)} %second.6), channel_id=1, source_target_pairs={{0,8},{4,12},{8,0},{12,4},{1,9},{5,13},{9,1},{13,5},{2,10},{6,14},... | collective-permute-start | bytes 1572872 | tf_op jit(solution)/shard_map/ppermute | solution.py:48
  159.8 26.3 %collective-permute-start.40 = (bf16[2,512,256]{2,1,0:T(8,128)(2,1)S(1)}, bf16[2,512,256]{2,1,0:T(8,128)(2,1)S(1)}, u32[]{:S(2)}, u32[]{:S(2)}) collective-permute-start(bf16[2,512,256]{2,1,0:T(8,128)(2,1)S(1)} %second.7), channel_id=1, source_target_pairs={{0,12},{4,8},{8,4},{12,0},{1,13},{5,9},{9,5},{13,1},{2,14},{6,10},... | collective-permute-start | bytes 1572872 | tf_op jit(solution)/shard_map/ppermute | solution.py:48
  162.8 27.7 %collective-permute-start.28 = (bf16[512,128]{1,0:T(8,128)(2,1)S(1)}, bf16[512,128]{1,0:T(8,128)(2,1)S(1)}, u32[]{:S(2)}, u32[]{:S(2)}) collective-permute-start(bf16[512,128]{1,0:T(8,128)(2,1)S(1)} %get-tuple-element.52), channel_id=1, source_target_pairs={{0,2},{1,3},{2,0},{3,1},{16,18},{17,19},{18,16},{19,17},{4,6},{5,7... | collective-permute-start | bytes 393224 | tf_op jit(solution)/shard_map/ppermute | solution.py:32
  166.3 25.8 %collective-permute-start.29 = (bf16[512,128]{1,0:T(8,128)(2,1)S(1)}, bf16[512,128]{1,0:T(8,128)(2,1)S(1)}, u32[]{:S(2)}, u32[]{:S(2)}) collective-permute-start(bf16[512,128]{1,0:T(8,128)(2,1)S(1)} %get-tuple-element.53), channel_id=1, source_target_pairs={{0,16},{1,17},{2,18},{3,19},{16,0},{17,1},{18,2},{19,3},{4,20},{5,... | collective-permute-start | bytes 393224 | tf_op jit(solution)/shard_map/ppermute | solution.py:32
  168.8 23.3 %collective-permute-start.30 = (bf16[512,128]{1,0:T(8,128)(2,1)S(1)}, bf16[512,128]{1,0:T(8,128)(2,1)S(1)}, u32[]{:S(2)}, u32[]{:S(2)}) collective-permute-start(bf16[512,128]{1,0:T(8,128)(2,1)S(1)} %get-tuple-element.54), channel_id=1, source_target_pairs={{0,18},{1,19},{2,16},{3,17},{16,2},{17,3},{18,0},{19,1},{4,22},{5,... | collective-permute-start | bytes 393224 | tf_op jit(solution)/shard_map/ppermute | solution.py:32
  (17 other events, 290.3 us)
where the time goes:
time: 203 us; the launch traced here: 200 us
  waiting for transfers between devices  103 us (51%)
  starting transfers between devices  69.9 us (34%)
  Pallas kernels  24.6 us (12%)
    ppermute x24, waiting for transfers between devices, permute_x(): return lax.ppermute(value, AX, pairs)  65.3 us
    ppermute x24, starting transfers between devices, permute_x(): return lax.ppermute(value, AX, pairs)  30.8 us
    ppermute x14, starting transfers between devices, shift_z(): return lax.ppermute(value, 'z', [(i, (i + s) % 8) for i in range(8)])  29.4 us
    ppermute x6, waiting for transfers between devices, xor_y(): return lax.ppermute(value, 'y', [(i, i ^ t) for i in range(4)])  27.8 us
    ppermute x6, starting transfers between devices, xor_y(): return lax.ppermute(value, 'y', [(i, i ^ t) for i in range(4)])  9.73 us
    ppermute x14, waiting for transfers between devices, shift_z(): return lax.ppermute(value, 'z', [(i, (i + s) % 8) for i in range(8)])  9.72 us
    pallas_call x4, Pallas kernels, second_product(): pl.pallas_call(functools.partial(second_kernel, order), out_shape=[shape(...  7.9 us
    pallas_call x3, Pallas kernels, first_product(): call(functools.partial(first_kernel, ks, len(carried)), [shape(2, 512, 25...  7.74 us
  transfers between devices with their start and end apart: 44, of which 23 were waited for; matrix products, arithmetic and copies ran while one was open for 0% of the time, Pallas kernels for 9%

commit v1 on v0

--- a/solution.py
+++ b/solution.py
@@ -12,7 +12,6 @@
 BF = jnp.bfloat16
 F32 = jnp.float32
 LIMIT = 24 << 20
-ROWS = 512
 VM = pl.BlockSpec(memory_space=pltpu.VMEM)
 SM = pl.BlockSpec(memory_space=pltpu.SMEM)
 ANY = pl.BlockSpec(memory_space=pl.ANY)
@@ -40,8 +39,8 @@
     return permute_x(value, lambda xh, xl, c: (xh, xl, 1 - c))
 
 
-def shift_z(value, s):
-    return lax.ppermute(value, "z", [(i, (i + s) % 8) for i in range(8)])
+def swap_z(value, side):
+    return lax.ppermute(value, "z", [(i, (((i - side) % 8 ^ 1) + side) % 8) for i in range(8)])
 
 
 def xor_y(value, t):
@@ -116,13 +115,12 @@
             outs[j][1, rows] = (invd[rows, lanes(q)] * keep).astype(BF)
 
 
-EVEN = ((0, 1), (6, 7), (2, 3), (4, 5))
-ODD = ((7, 0), (1, 2), (5, 6), (3, 4))
+PAIRS = (((0, 0), (0, 1)), ((1, 2), (1, 1)), ((0, 2), (0, 3)), ((0, 4), (1, 3)))
 
 
 def first_kernel(ks, count, idx, *refs):
-    pairs = [refs[8 * i : 8 * i + 8] for i in range(len(ks))]
-    refs = refs[8 * len(ks) :]
+    pairs = [refs[4 * i : 4 * i + 4] for i in range(len(ks))]
+    refs = refs[4 * len(ks) :]
     left, rest = refs[:4], refs[4]
     sends, wv, outv, osem = (lambda r: (r[:4], *r[4:]))(refs[5 + count :])
     _, c, xh, _, z, y = placed(idx)
@@ -134,20 +132,20 @@
         return pltpu.make_async_copy(outv.at[i], sends[t], osem.at[i])
 
     for i in range(len(ks)):
-        for odd in range(2):
-
-            @pl.when(odd_z == odd)
-            def _(i=i, odd=odd):
-                for e in range(2):
-                    for a in range(2):
-                        wv[a, :, e * 128 : e * 128 + 128] = pairs[i][odd * 4 + e * 2 + a][...]
-
-        for half in range(2):
-            own = jnp.concatenate([left[half * 2][...], left[half * 2 + 1][...]], 1)
-            other = jnp.concatenate([rest[half * 2], rest[half * 2 + 1]], 1)
-            total = jnp.dot(own, wv[flip], preferred_element_type=F32)
-            total += jnp.dot(other, wv[1 - flip], preferred_element_type=F32)
-            outv[i, xh ^ half] = total.astype(BF)
+        for at in range(2):
+            for a in range(2):
+                wv[a, :, lanes(at ^ odd_z)] = pairs[i][at * 2 + a][...]
+
+        @pl.loop(0, 2)
+        def _(r, i=i):
+            rows = pl.ds(pl.multiple_of(r * 256, 256), 256)
+            for half in range(2):
+                own = jnp.concatenate([left[half * 2][rows], left[half * 2 + 1][rows]], 1)
+                other = jnp.concatenate([rest[half * 2, rows], rest[half * 2 + 1, rows]], 1)
+                total = jnp.dot(own, wv[flip], preferred_element_type=F32)
+                total += jnp.dot(other, wv[1 - flip], preferred_element_type=F32)
+                outv[i, xh ^ half, rows] = total.astype(BF)
+
         for t in range(4):
 
             @pl.when((dests[i] ^ y) == t)
@@ -159,7 +157,7 @@
 
 
 def first_product(ks, idx, pieces, left, carried):
-    group = [pieces[a][s] for k in ks for pairs in (EVEN[k], ODD[k]) for s in pairs for a in range(2)]
+    group = [pieces[a][at] for k in ks for at in PAIRS[k] for a in range(2)]
     return call(
         functools.partial(first_kernel, ks, len(carried)),
         [shape(2, 512, 256)] * 4,
@@ -176,13 +174,17 @@
     )(idx, *group, *left, *carried)
 
 
+ORDER = tuple(at for pair in PAIRS for at in pair)
+
+
 def arrange(idx, *refs):
     d, c, xh, xl, z, _ = placed(idx)
     out = refs[16]
+    up = 1 - 2 * (z & 1)
     for a in range(2):
-        for s in range(8):
+        for s, (side, step) in enumerate(ORDER):
             piece = refs[a * 8 + s]
-            owner = (z + s) & 7
+            owner = (z + (1 - 2 * side) * step * up) & 7
 
             @pl.loop(0, 8)
             def _(block, a=a, piece=piece, owner=owner):
@@ -192,38 +194,38 @@
                 out[owner >> 1, rows, lanes(owner & 1)] = piece[pl.ds(pl.multiple_of(block * 128, 128), 128)]
 
 
-def second_kernel(order, idx, *refs):
-    left, weights, outs = refs[:8], refs[8], refs[9:]
-
-    @pl.loop(0, 2)
-    def _(h):
-        whole = jnp.concatenate([ref[h] for ref in left], 1)
-        got = jnp.dot(whole, weights[...], preferred_element_type=F32).astype(BF)
-        for i in range(len(order)):
-
-            @pl.when(pl.program_id(0) == i)
-            def _(i=i):
-                outs[i][h] = got
+def join_b(one, two, three, out):
+    out[0] = one[...]
+    out[1] = two[...]
+    out[2] = three[...]
+
+
+def second_kernel(idx, *refs):
+    own, swapped, joined, weights, out = refs[:4], refs[4], refs[5], refs[6], refs[7]
+    left = [ref[...] for ref in own] + [swapped[...]] + [joined[i] for i in range(3)]
+    left = jnp.concatenate([v.reshape(512, 256) for v in left], 1)
+    out[...] = jnp.dot(left, weights[...], preferred_element_type=F32).astype(BF).reshape(2, 256, 256)
 
 
 def second_product(t, idx, left, w_all):
-    order = (t,)
-    whole = pl.BlockSpec((2, ROWS, 256), lambda i, s: (0, 0, 0))
+    whole = pl.BlockSpec((2, 256, 256), lambda i, s: (0, 0, 0))
     return pl.pallas_call(
-        functools.partial(second_kernel, order),
-        out_shape=[shape(2, ROWS, 256)] * len(order),
+        second_kernel,
+        out_shape=shape(2, 256, 256),
         grid_spec=pltpu.PrefetchScalarGridSpec(
             num_scalar_prefetch=1,
-            grid=(len(order),),
-            in_specs=[whole] * 8 + [pl.BlockSpec((None, 2048, 256), lambda i, s: (placed(s)[5] ^ t, 0, 0))],
-            out_specs=[whole] * len(order),
+            grid=(1,),
+            in_specs=[whole] * 5
+            + [
+                pl.BlockSpec((3, 2, 256, 256), lambda i, s: (0, 0, 0, 0)),
+                pl.BlockSpec((None, 2048, 256), lambda i, s: (placed(s)[5] ^ t, 0, 0)),
+            ],
+            out_specs=whole,
         ),
         name="second",
         compiler_params=pltpu.CompilerParams(vmem_limit_bytes=LIMIT),
-        cost_estimate=pl.CostEstimate(
-            flops=2 * 2 * ROWS * 2048 * 256 * len(order), bytes_accessed=(2 + len(order)) << 20, transcendentals=0
-        ),
-    )(idx, *left, w_all)[0]
+        cost_estimate=pl.CostEstimate(flops=2 * 512 * 2048 * 256, bytes_accessed=2 << 20, transcendentals=0),
+    )(idx, *left, w_all)
 
 
 def summed(parts, h, e, rows):
@@ -234,50 +236,53 @@
 
 
 def update_kernel(idx, *refs):
-    parts, left, terms, nxt, outs = refs[:4], refs[4:8], refs[8:12], refs[-5], refs[-4:]
+    parts, left, terms, nxt, outs = refs[:4], refs[4:8], refs[8:12], refs[12:14], refs[14:]
     d = placed(idx)[0]
 
-    @pl.loop(0, 4)
-    def _(i):
-        rows = lanes(i)
-        for j in range(4):
-            h, e = (d ^ j) >> 1, (d ^ j) & 1
-            ladder = summed(parts, h, e, rows)
-            outs[j][rows] = ladder.astype(BF)
-            step = terms[j][1, rows].astype(F32) * (terms[j][0, rows].astype(F32) + ladder)
-            nxt[h, rows, lanes(e)] = (left[j][rows].astype(F32) - step).astype(BF)
-
-
-def update(n, idx, parts, left, terms, carried):
-    whole = pl.BlockSpec((2, ROWS, 256), lambda i, s: (0, 0, 0))
-    quarter = pl.BlockSpec((ROWS, 128), lambda i, s: (n, 0))
+    for n in range(2):
+
+        @pl.loop(0, 2)
+        def _(i, n=n):
+            rows = lanes(2 * n + i)
+            for j in range(4):
+                h, e = (d ^ j) >> 1, (d ^ j) & 1
+                ladder = summed(parts, h, e, rows)
+                outs[j][rows] = ladder.astype(BF)
+                step = terms[j][1, rows].astype(F32) * (terms[j][0, rows].astype(F32) + ladder)
+                nxt[n][h, lanes(i), lanes(e)] = (left[j][rows].astype(F32) - step).astype(BF)
+
+
+def update(idx, parts, left, terms):
+    whole = pl.BlockSpec((2, 512, 256), lambda i, s: (0, 0, 0))
+    half = pl.BlockSpec((2, 256, 256), lambda i, s: (0, 0, 0))
+    quarter = pl.BlockSpec((512, 128), lambda i, s: (0, 0))
     return pl.pallas_call(
         update_kernel,
-        out_shape=[shape(2, ROWS, 256)] + [shape(512, 128)] * 4,
+        out_shape=[shape(2, 256, 256)] * 2 + [shape(512, 128)] * 4,
         grid_spec=pltpu.PrefetchScalarGridSpec(
             num_scalar_prefetch=1,
             grid=(1,),
             in_specs=[whole] * 4
-            + [pl.BlockSpec((ROWS, 128), lambda i, s: (n, placed(s)[0]))] * 4
-            + [pl.BlockSpec((2, ROWS, 128), lambda i, s: (0, n, 0))] * 4
-            + [ANY] * len(carried),
-            out_specs=[whole] + [quarter] * 4,
+            + [pl.BlockSpec((512, 128), lambda i, s: (0, placed(s)[0]))] * 4
+            + [pl.BlockSpec((2, 512, 128), lambda i, s: (0, 0, 0))] * 4,
+            out_specs=[half] * 2 + [quarter] * 4,
         ),
+        name="update",
         compiler_params=pltpu.CompilerParams(vmem_limit_bytes=LIMIT),
         cost_estimate=pl.CostEstimate(flops=0, bytes_accessed=2 << 20, transcendentals=0),
-        input_output_aliases={13 + i: 1 + i for i in range(len(carried))},
-    )(idx, *parts, *left, *terms, *carried)
+    )(idx, *parts, *left, *terms)
 
 
 def sum_kernel(idx, *refs):
     parts, outs = refs[:-4], refs[-4:]
     d = placed(idx)[0]
-
-    @pl.loop(0, 4)
-    def _(i):
-        rows = lanes(i)
-        for j in range(4):
-            outs[j][rows] = summed(parts, (d ^ j) >> 1, (d ^ j) & 1, rows).astype(BF)
+    for n in range(2):
+
+        @pl.loop(0, 2)
+        def _(i, n=n):
+            for j in range(4):
+                ladder = summed(parts[n * 4 : n * 4 + 4], (d ^ j) >> 1, (d ^ j) & 1, lanes(i))
+                outs[j][lanes(2 * n + i)] = ladder.astype(BF)
 
 
 def final_kernel(idx, amps, base, invd, *refs):
@@ -312,16 +317,15 @@
     masked = call(prep_a, shape(512, 512), [SM, VM], VM)(idx, amps)
     terms = call(prep_t, [shape(2, 512, 128)] * 4, [SM, VM, VM], [VM] * 4)(idx, base, invd)
 
-    pieces = [[own[0]] + [None] * 7, [own[1]] + [None] * 7]
-    up, down = list(own), list(own)
+    pieces = [{(0, 0): own[g]} for g in range(2)]
+    sent = [[v, v] for v in own]
     for step in range(1, 4):
         for g in range(2):
-            up[g] = shift_z(up[g], 1)
-            down[g] = shift_z(down[g], -1)
-            pieces[g][8 - step] = up[g]
-            pieces[g][step] = down[g]
-    pieces[0][4] = shift_z(up[0], 1)
-    pieces[1][4] = shift_z(down[1], -1)
+            for side in range(2):
+                pieces[g][side, step] = swap_z(sent[g][side], side)
+            sent[g] = [pieces[g][1, step], pieces[g][0, step]]
+    pieces[0][0, 4] = swap_z(sent[0][0], 0)
+    pieces[1][0, 4] = swap_z(sent[1][1], 1)
 
     left = [masked]
     for j in range(1, 4):
@@ -335,7 +339,9 @@
     sends = first_product((0, 1), idx, pieces, left, [])
     sends = first_product((2,), idx, pieces, left, sends)
     sends = first_product((3,), idx, pieces, left, sends)
-    w_all = call(arrange, shape(4, 2048, 256), [SM] + [VM] * 16, VM, moved=8 << 20)(idx, *pieces[0], *pieces[1])
+    w_all = call(arrange, shape(4, 2048, 256), [SM] + [VM] * 16, VM, moved=8 << 20)(
+        idx, *(pieces[g][at] for g in range(2) for at in ORDER)
+    )
 
     def reduced(sends):
         got = [sends[0]] + [None] * 3
@@ -349,15 +355,19 @@
             got[j] = chip_xor(values[j], j)
         return got
 
-    nxt, *ladder = update(0, idx, reduced(sends), left[:4], terms, [])
-    chips = spread([nxt] * 4)
-    chips = chips + [core_swap(v) for v in chips]
-    parts = [None] * 4
-    for t in (2, 1, 3, 0):
-        parts[t] = second_product(t, idx, chips, w_all)
-    parts = reduced(parts)
-    first = spread(ladder)
-    ladder = call(sum_kernel, [shape(512, 128)] * 4, [SM] + [VM] * 4, [VM] * 4)(idx, *parts)
+    *nxt, l0, l1, l2, l3 = update(idx, reduced(sends), left[:4], terms)
+    first = spread([l0, l1, l2, l3])
+    parts = []
+    for n in range(2):
+        chips = spread([nxt[n]] * 4)
+        chips.append(core_swap(nxt[n]))
+        joined = call(join_b, shape(3, 2, 256, 256), [VM] * 3, VM)(*chips[1:4])
+        chips.append(core_swap(joined))
+        got = [None] * 4
+        for t in (2, 1, 3, 0):
+            got[t] = second_product(t, idx, chips, w_all)
+        parts += reduced(got)
+    ladder = call(sum_kernel, [shape(512, 128)] * 4, [SM] + [VM] * 8, [VM] * 4)(idx, *parts)
     second = spread(ladder)
     return call(
         final_kernel, [shape(512, 512), shape(512, 512, dtype=F32)], [SM] + [VM] * 11, [VM] * 2, moved=6 << 20

time: 203 us -> 196 us (0.966)
  waiting for transfers between devices: 103 us -> 89.2 us
  starting transfers between devices: 69.9 us -> 73.7 us
  Pallas kernels: 24.6 us -> 27.5 us
    ppermute x6 -> x9, waiting for transfers between devices: 27.8 us -> 17.6 us  [xor_y(): return lax.ppermute(value, 'y', [(i, i ^ t) for i in range(4)])]
    ppermute x24 -> x27, waiting for transfers between devices: 65.3 us -> 57.7 us  [permute_x(): return lax.ppermute(value, AX, pairs)]
    ppermute x24 -> x27, starting transfers between devices: 30.8 us -> 38.1 us  [permute_x(): return lax.ppermute(value, AX, pairs)]
    ppermute x14, starting transfers between devices: 29.4 us -> 24.2 us  [swap_z(): lax.ppermute(value, 'z', [(i, (((i - side) % 8 ^ 1) + side) % 8) for i in...]
    ppermute x14, waiting for transfers between devices: 9.72 us -> 13.9 us  [swap_z(): lax.ppermute(value, 'z', [(i, (((i - side) % 8 ^ 1) + side) % 8) for i in...]
    pallas_call x6 -> x12, Pallas kernels: 9.93 us -> 12.2 us  [the longest x8 10.1 us: second_product(): pl.pallas_call(second_kernel, out_shape=shape(2, 256, 256), grid_spec=plt...]
    ppermute x6 -> x9, starting transfers between devices: 9.73 us -> 11.4 us  [xor_y(): return lax.ppermute(value, 'y', [(i, i ^ t) for i in range(4)])]
  transfers between devices with their start and end apart: 44 -> 50, of which waited for: 23 -> 25; matrix products, arithmetic and copies ran while one was open for 0% -> 0% of each run, Pallas kernels for 9% -> 12%
where the time goes in v1:
time: 196 us; the launch traced here: 193 us
  waiting for transfers between devices  89.2 us (46%)
  starting transfers between devices  73.7 us (38%)
  Pallas kernels  27.5 us (14%)
    ppermute x27, waiting for transfers between devices, permute_x(): return lax.ppermute(value, AX, pairs)  57.7 us
    ppermute x27, starting transfers between devices, permute_x(): return lax.ppermute(value, AX, pairs)  38.1 us
    ppermute x14, starting transfers between devices, swap_z(): lax.ppermute(value, 'z', [(i, (((i - side) % 8 ^ 1) + side) % 8) for i in...  24.2 us
    ppermute x9, waiting for transfers between devices, xor_y(): return lax.ppermute(value, 'y', [(i, i ^ t) for i in range(4)])  17.6 us
    ppermute x14, waiting for transfers between devices, swap_z(): lax.ppermute(value, 'z', [(i, (((i - side) % 8 ^ 1) + side) % 8) for i in...  13.9 us
    ppermute x9, starting transfers between devices, xor_y(): return lax.ppermute(value, 'y', [(i, i ^ t) for i in range(4)])  11.4 us
    pallas_call x8, Pallas kernels, second_product(): pl.pallas_call(second_kernel, out_shape=shape(2, 256, 256), grid_spec=plt...  10.1 us
    pallas_call x3, Pallas kernels, first_product(): call(functools.partial(first_kernel, ks, len(carried)), [shape(2, 512, 25...  8.38 us
  transfers between devices with their start and end apart: 50, of which 25 were waited for; matrix products, arithmetic and copies ran while one was open for 0% of the time, Pallas kernels for 12%

profile of v1, /device:TPU:4, one launch (start us, length us, event | category | flops | bytes accessed | tf_op | source)
XLA Modules:
  0.0 193.2 jit_solution(4845153219223280067)
XLA Ops:
  6.6 11.3 %collective-permute-done.15.one.refs_9_.refs_5_ = bf16[512,512]{1,0:T(8,128)(2,1)S(1)} collective-permute-done((bf16[512,512]{1,0:T(8,128)(2,1)S(1)}, bf16[512,512]{1,0:T(8,128)(2,1)S(1)}, u32[]{:S(2)}, u32[]{:S(2)}) %collective-permute-start.15) | collective-permute-done | bytes 524320 | tf_op jit(solution)/shard_map/ppermute | solution.py:31
  17.9 10.2 %collective-permute-done.16.two.refs_10_.refs_6_ = bf16[512,512]{1,0:T(8,128)(2,1)S(1)} collective-permute-done((bf16[512,512]{1,0:T(8,128)(2,1)S(1)}, bf16[512,512]{1,0:T(8,128)(2,1)S(1)}, u32[]{:S(2)}, u32[]{:S(2)}) %collective-permute-start.16) | collective-permute-done | bytes 524320 | tf_op jit(solution)/shard_map/ppermute | solution.py:31
  30.9 2.9 %collective-permute-start.7 = (bf16[512,128]{1,0:T(8,128)(2,1)S(1)}, bf16[512,128]{1,0:T(8,128)(2,1)S(1)}, u32[]{:S(2)}, u32[]{:S(2)}) collective-permute-start(bf16[512,128]{1,0:T(8,128)(2,1)S(1)} %get-tuple-element.35), channel_id=1, source_target_pairs={{0,18},{1,2},{2,16},{3,0},{16,19},{17,3},{18,17},{19,1},{4,22},{5,... | collective-permute-start | bytes 393224 | tf_op jit(solution)/shard_map/ppermute | solution.py:31
  33.8 3.4 %collective-permute-start = (bf16[512,128]{1,0:T(8,128)(2,1)S(1)}, bf16[512,128]{1,0:T(8,128)(2,1)S(1)}, u32[]{:S(2)}, u32[]{:S(2)}) collective-permute-start(bf16[512,128]{1,0:T(8,128)(2,1)S(1)} %get-tuple-element.32), channel_id=1, source_target_pairs={{0,0},{1,16},{2,2},{3,18},{16,1},{17,17},{18,3},{19,19},{4,4},{5,2... | collective-permute-start | bytes 393224 | tf_op jit(solution)/shard_map/ppermute | solution.py:31
  43.0 5.9 %collective-permute-start.2 = (bf16[1024,128]{1,0:T(8,128)(2,1)S(1)}, bf16[1024,128]{1,0:T(8,128)(2,1)S(1)}, u32[]{:S(2)}, u32[]{:S(2)}) collective-permute-start(bf16[1024,128]{1,0:T(8,128)(2,1)S(1)} %shard_map.87.refs_0_), channel_id=1, source_target_pairs={{0,224},{32,64},{64,32},{96,128},{128,96},{160,192},{192,160},{224... | collective-permute-start | bytes 786440 | tf_op jit(solution)/shard_map/ppermute | solution.py:43
  51.0 3.4 %collective-permute-start.9 = (bf16[1024,128]{1,0:T(8,128)(2,1)S(1)}, bf16[1024,128]{1,0:T(8,128)(2,1)S(1)}, u32[]{:S(2)}, u32[]{:S(2)}) collective-permute-start(bf16[1024,128]{1,0:T(8,128)(2,1)S(1)} %collective-permute-done.8.refs_3_.refs_9_), channel_id=1, source_target_pairs={{0,224},{32,64},{64,32},{96,128},{128,96},{160,192},{192,160},{224... | collective-permute-start | bytes 786440 | tf_op jit(solution)/shard_map/ppermute | solution.py:43
  56.1 3.9 %collective-permute-start.20 = (bf16[1024,128]{1,0:T(8,128)(2,1)S(1)}, bf16[1024,128]{1,0:T(8,128)(2,1)S(1)}, u32[]{:S(2)}, u32[]{:S(2)}) collective-permute-start(bf16[1024,128]{1,0:T(8,128)(2,1)S(1)} %collective-permute-done.19.refs_2_.refs_1_), channel_id=1, source_target_pairs={{0,224},{32,64},{64,32},{96,128},{128,96},{160,192},{192,160},{224... | collective-permute-start | bytes 786440 | tf_op jit(solution)/shard_map/ppermute | solution.py:43
  61.7 5.6 %collective-permute-done.9.refs_5_.refs_10_ = bf16[1024,128]{1,0:T(8,128)(2,1)S(1)} collective-permute-done((bf16[1024,128]{1,0:T(8,128)(2,1)S(1)}, bf16[1024,128]{1,0:T(8,128)(2,1)S(1)}, u32[]{:S(2)}, u32[]{:S(2)}) %collective-permute-start.9) | collective-permute-done | bytes 262176 | tf_op jit(solution)/shard_map/ppermute | solution.py:43
  67.4 3.2 %collective-permute-start.4 = (bf16[1024,128]{1,0:T(8,128)(2,1)S(1)}, bf16[1024,128]{1,0:T(8,128)(2,1)S(1)}, u32[]{:S(2)}, u32[]{:S(2)}) collective-permute-start(bf16[1024,128]{1,0:T(8,128)(2,1)S(1)} %collective-permute-done.3.refs_0_.refs_4_), channel_id=1, source_target_pairs={{0,224},{32,64},{64,32},{96,128},{128,96},{160,192},{192,160},{224... | collective-permute-start | bytes 786440 | tf_op jit(solution)/shard_map/ppermute | solution.py:43
  70.6 2.4 %collective-permute-done.20.refs_4_.refs_2_ = bf16[1024,128]{1,0:T(8,128)(2,1)S(1)} collective-permute-done((bf16[1024,128]{1,0:T(8,128)(2,1)S(1)}, bf16[1024,128]{1,0:T(8,128)(2,1)S(1)}, u32[]{:S(2)}, u32[]{:S(2)}) %collective-permute-start.20) | collective-permute-done | bytes 262176 | tf_op jit(solution)/shard_map/ppermute | solution.py:43
  76.5 3.2 %collective-permute-start.14 = (bf16[1024,128]{1,0:T(8,128)(2,1)S(1)}, bf16[1024,128]{1,0:T(8,128)(2,1)S(1)}, u32[]{:S(2)}, u32[]{:S(2)}) collective-permute-start(bf16[1024,128]{1,0:T(8,128)(2,1)S(1)} %collective-permute-done.13.refs_1_.refs_12_), channel_id=1, source_target_pairs={{0,224},{32,64},{64,32},{96,128},{128,96},{160,192},{192,160},{224... | collective-permute-start | bytes 786440 | tf_op jit(solution)/shard_map/ppermute | solution.py:43
  80.2 3.9 %shard_map.91 = (bf16[2,512,256]{2,1,0:T(8,128)(2,1)S(1)}, bf16[2,512,256]{2,1,0:T(8,128)(2,1)S(1)}, bf16[2,512,256]{2,1,0:T(8,128)(2,1)S(1)}, bf16[2,512,256]{2,1,0:T(8,128)(2,1)S(1)}) custom-call(s32[2,2]{1,0:T(2,128)S(1)} %or_or_fusion.idx, bf16[1024,128]{1,0:T(8,128)(2,1)S(1)} %shard_map.87.refs_0_, bf16[1024,128]{1,0:T(8,128)(2,1)S(1)} %shard_map.88.refs_1_.refs_8_, ...), custom_call_target="tpu_custom_call" | custom-call | flops 2147483648 | bytes 2097152 | tf_op jit(solution)/shard_map/pallas_call | solution.py:161
  91.4 2.9 %collective-permute-start.23 = (bf16[2,512,256]{2,1,0:T(8,128)(2,1)S(1)}, bf16[2,512,256]{2,1,0:T(8,128)(2,1)S(1)}, u32[]{:S(2)}, u32[]{:S(2)}) collective-permute-start(bf16[2,512,256]{2,1,0:T(8,128)(2,1)S(1)} %get-tuple-element.46), channel_id=1, source_target_pairs={{0,8},{4,12},{8,0},{12,4},{1,9},{5,13},{9,1},{13,5},{2,10},{6,14},... | collective-permute-start | bytes 1572872 | tf_op jit(solution)/shard_map/ppermute | solution.py:47
  94.5 3.7 %collective-permute-start.27 = (bf16[2,512,128]{2,1,0:T(8,128)(2,1)S(1)}, bf16[2,512,128]{2,1,0:T(8,128)(2,1)S(1)}, u32[]{:S(2)}, u32[]{:S(2)}) collective-permute-start(bf16[2,512,128]{2,1,0:T(8,128)(2,1)S(1)} %get-tuple-element.51), channel_id=1, source_target_pairs={{0,18},{1,19},{2,16},{3,17},{16,2},{17,3},{18,0},{19,1},{4,22},{5,... | collective-permute-start | bytes 786440 | tf_op jit(solution)/shard_map/ppermute | solution.py:31
  98.3 4.1 %collective-permute-done.26.refs_10_ = bf16[2,512,128]{2,1,0:T(8,128)(2,1)S(1)} collective-permute-done((bf16[2,512,128]{2,1,0:T(8,128)(2,1)S(1)}, bf16[2,512,128]{2,1,0:T(8,128)(2,1)S(1)}, u32[]{:S(2)}, u32[]{:S(2)}) %collective-permute-start.26) | collective-permute-done | bytes 262176 | tf_op jit(solution)/shard_map/ppermute | solution.py:31
  102.4 5.2 %collective-permute-done.27.refs_11_ = bf16[2,512,128]{2,1,0:T(8,128)(2,1)S(1)} collective-permute-done((bf16[2,512,128]{2,1,0:T(8,128)(2,1)S(1)}, bf16[2,512,128]{2,1,0:T(8,128)(2,1)S(1)}, u32[]{:S(2)}, u32[]{:S(2)}) %collective-permute-start.27) | collective-permute-done | bytes 262176 | tf_op jit(solution)/shard_map/ppermute | solution.py:31
  107.6 4.9 %collective-permute-done.23.refs_2_ = bf16[2,512,256]{2,1,0:T(8,128)(2,1)S(1)} collective-permute-done((bf16[2,512,256]{2,1,0:T(8,128)(2,1)S(1)}, bf16[2,512,256]{2,1,0:T(8,128)(2,1)S(1)}, u32[]{:S(2)}, u32[]{:S(2)}) %collective-permute-start.23) | collective-permute-done | bytes 524320 | tf_op jit(solution)/shard_map/ppermute | solution.py:47
  112.5 2.7 %collective-permute-done.24.refs_3_ = bf16[2,512,256]{2,1,0:T(8,128)(2,1)S(1)} collective-permute-done((bf16[2,512,256]{2,1,0:T(8,128)(2,1)S(1)}, bf16[2,512,256]{2,1,0:T(8,128)(2,1)S(1)}, u32[]{:S(2)}, u32[]{:S(2)}) %collective-permute-start.24) | collective-permute-done | bytes 524320 | tf_op jit(solution)/shard_map/ppermute | solution.py:47
  117.4 3.5 %collective-permute-start.40 = (bf16[2,256,256]{2,1,0:T(8,128)(2,1)S(1)}, bf16[2,256,256]{2,1,0:T(8,128)(2,1)S(1)}, u32[]{:S(2)}, u32[]{:S(2)}) collective-permute-start(bf16[2,256,256]{2,1,0:T(8,128)(2,1)S(1)} %get-tuple-element.57.refs_0_), channel_id=1, source_target_pairs={{0,16},{1,17},{2,18},{3,19},{16,0},{17,1},{18,2},{19,3},{4,20},{5,... | collective-permute-start | bytes 786440 | tf_op jit(solution)/shard_map/ppermute | solution.py:31
  124.4 3.9 %collective-permute-start.33 = (bf16[2,256,256]{2,1,0:T(8,128)(2,1)S(1)}, bf16[2,256,256]{2,1,0:T(8,128)(2,1)S(1)}, u32[]{:S(2)}, u32[]{:S(2)}) collective-permute-start(bf16[2,256,256]{2,1,0:T(8,128)(2,1)S(1)} %get-tuple-element.56.refs_0_), channel_id=1, source_target_pairs={{0,18},{1,19},{2,16},{3,17},{16,2},{17,3},{18,0},{19,1},{4,22},{5,... | collective-permute-start | bytes 786440 | tf_op jit(solution)/shard_map/ppermute | solution.py:31
  128.3 5.2 %collective-permute-done.40.two.refs_2_ = bf16[2,256,256]{2,1,0:T(8,128)(2,1)S(1)} collective-permute-done((bf16[2,256,256]{2,1,0:T(8,128)(2,1)S(1)}, bf16[2,256,256]{2,1,0:T(8,128)(2,1)S(1)}, u32[]{:S(2)}, u32[]{:S(2)}) %collective-permute-start.40) | collective-permute-done | bytes 262176 | tf_op jit(solution)/shard_map/ppermute | solution.py:31
  133.5 2.3 %collective-permute-done.41.three.refs_3_ = bf16[2,256,256]{2,1,0:T(8,128)(2,1)S(1)} collective-permute-done((bf16[2,256,256]{2,1,0:T(8,128)(2,1)S(1)}, bf16[2,256,256]{2,1,0:T(8,128)(2,1)S(1)}, u32[]{:S(2)}, u32[]{:S(2)}) %collective-permute-start.41) | collective-permute-done | bytes 262176 | tf_op jit(solution)/shard_map/ppermute | solution.py:31
  135.9 8.9 %collective-permute-done.32.two.refs_2_ = bf16[2,256,256]{2,1,0:T(8,128)(2,1)S(1)} collective-permute-done((bf16[2,256,256]{2,1,0:T(8,128)(2,1)S(1)}, bf16[2,256,256]{2,1,0:T(8,128)(2,1)S(1)}, u32[]{:S(2)}, u32[]{:S(2)}) %collective-permute-start.32) | collective-permute-done | bytes 262176 | tf_op jit(solution)/shard_map/ppermute | solution.py:31
  147.7 2.3 %shard_map.96.refs_6_ = bf16[4,2048,256]{2,1,0:T(8,128)(2,1)S(1)} custom-call(s32[2,2]{1,0:T(2,128)S(1)} %or_or_fusion.idx, bf16[1024,128]{1,0:T(8,128)(2,1)S(1)} %shard_map.87.refs_0_, bf16[1024,128]{1,0:T(8,128)(2,1)S(1)} %collective-permute-done.19.refs_2_.refs_1_, bf16[1024,128]{1,0:T(8,128)(2,1)S(1)} %collective-permute-done.20.refs_4_.refs_2_, ...), custom_call_target="tpu_custom_call" | custom-call | bytes 8388608 | tf_op jit(solution)/shard_map/pallas_call | solution.py:342
  155.0 3.2 %collective-permute-start.44 = (bf16[2,256,256]{2,1,0:T(8,128)(2,1)S(1)}, bf16[2,256,256]{2,1,0:T(8,128)(2,1)S(1)}, u32[]{:S(2)}, u32[]{:S(2)}) collective-permute-start(bf16[2,256,256]{2,1,0:T(8,128)(2,1)S(1)} %second.13), channel_id=1, source_target_pairs={{0,4},{4,0},{8,12},{12,8},{1,5},{5,1},{9,13},{13,9},{2,6},{6,2},{1... | collective-permute-start | bytes 786440 | tf_op jit(solution)/shard_map/ppermute | solution.py:47
  164.3 3.1 %collective-permute-done.46.refs_7_ = bf16[2,256,256]{2,1,0:T(8,128)(2,1)S(1)} collective-permute-done((bf16[2,256,256]{2,1,0:T(8,128)(2,1)S(1)}, bf16[2,256,256]{2,1,0:T(8,128)(2,1)S(1)}, u32[]{:S(2)}, u32[]{:S(2)}) %collective-permute-start.46) | collective-permute-done | bytes 262176 | tf_op jit(solution)/shard_map/ppermute | solution.py:47
  167.4 2.7 %collective-permute-start.28 = (bf16[512,128]{1,0:T(8,128)(2,1)S(1)}, bf16[512,128]{1,0:T(8,128)(2,1)S(1)}, u32[]{:S(2)}, u32[]{:S(2)}) collective-permute-start(bf16[512,128]{1,0:T(8,128)(2,1)S(1)} %get-tuple-element.53), channel_id=1, source_target_pairs={{0,2},{1,3},{2,0},{3,1},{16,18},{17,19},{18,16},{19,17},{4,6},{5,7... | collective-permute-start | bytes 393224 | tf_op jit(solution)/shard_map/ppermute | solution.py:31
  172.8 5.0 %collective-permute-done.38.refs_3_ = bf16[2,256,256]{2,1,0:T(8,128)(2,1)S(1)} collective-permute-done((bf16[2,256,256]{2,1,0:T(8,128)(2,1)S(1)}, bf16[2,256,256]{2,1,0:T(8,128)(2,1)S(1)}, u32[]{:S(2)}, u32[]{:S(2)}) %collective-permute-start.38) | collective-permute-done | bytes 262176 | tf_op jit(solution)/shard_map/ppermute | solution.py:47
  180.7 2.8 %collective-permute-start.47 = (bf16[512,128]{1,0:T(8,128)(2,1)S(1)}, bf16[512,128]{1,0:T(8,128)(2,1)S(1)}, u32[]{:S(2)}, u32[]{:S(2)}) collective-permute-start(bf16[512,128]{1,0:T(8,128)(2,1)S(1)} %get-tuple-element.59), channel_id=1, source_target_pairs={{0,2},{1,3},{2,0},{3,1},{16,18},{17,19},{18,16},{19,17},{4,6},{5,7... | collective-permute-start | bytes 393224 | tf_op jit(solution)/shard_map/ppermute | solution.py:31
  185.1 2.3 %collective-permute-done.47.refs_5_ = bf16[512,128]{1,0:T(8,128)(2,1)S(1)} collective-permute-done((bf16[512,128]{1,0:T(8,128)(2,1)S(1)}, bf16[512,128]{1,0:T(8,128)(2,1)S(1)}, u32[]{:S(2)}, u32[]{:S(2)}) %collective-permute-start.47) | collective-permute-done | bytes 131104 | tf_op jit(solution)/shard_map/ppermute | solution.py:31
  187.4 2.7 %collective-permute-done.48.refs_6_ = bf16[512,128]{1,0:T(8,128)(2,1)S(1)} collective-permute-done((bf16[512,128]{1,0:T(8,128)(2,1)S(1)}, bf16[512,128]{1,0:T(8,128)(2,1)S(1)}, u32[]{:S(2)}, u32[]{:S(2)}) %collective-permute-start.48) | collective-permute-done | bytes 131104 | tf_op jit(solution)/shard_map/ppermute | solution.py:31
  190.8 2.4 %shard_map.99 = (bf16[512,512]{1,0:T(8,128)(2,1)}, f32[512,512]{1,0:T(8,128)}) custom-call(s32[2,2]{1,0:T(2,128)S(1)} %or_or_fusion.idx, bf16[512,512]{1,0:T(8,128)(2,1)S(1)} %copy-done.3, f32[512,512]{1,0:T(8,128)S(1)} %copy-done, f32[512,512]{1,0:T(8,128)S(1)} %copy-done.1, bf16[512,128]{1,0:T(8,128)(2,1)S(1)} %get-tuple-element.52.refs_0_, ...), custom_call_target="tpu_custom_call" | custom-call | bytes 6291456 | tf_op jit(solution)/shard_map/pallas_call | solution.py:372
  (102 shorter events, 59.0 us)
Async XLA Ops:
  3.0 14.9 %collective-permute-start.15 = (bf16[512,512]{1,0:T(8,128)(2,1)S(1)}, bf16[512,512]{1,0:T(8,128)(2,1)S(1)}, u32[]{:S(2)}, u32[]{:S(2)}) collective-permute-start(bf16[512,512]{1,0:T(8,128)(2,1)S(1)} %shard_map.89.zero.refs_8_.refs_4_), channel_id=1, source_target_pairs={{0,2},{1,3},{2,0},{3,1},{16,18},{17,19},{18,16},{19,17},{4,6},{5,7... | collective-permute-start | bytes 1572872 | tf_op jit(solution)/shard_map/ppermute | solution.py:31
  4.3 23.8 %collective-permute-start.16 = (bf16[512,512]{1,0:T(8,128)(2,1)S(1)}, bf16[512,512]{1,0:T(8,128)(2,1)S(1)}, u32[]{:S(2)}, u32[]{:S(2)}) collective-permute-start(bf16[512,512]{1,0:T(8,128)(2,1)S(1)} %shard_map.89.zero.refs_8_.refs_4_), channel_id=1, source_target_pairs={{0,16},{1,17},{2,18},{3,19},{16,0},{17,1},{18,2},{19,3},{4,20},{5,... | collective-permute-start | bytes 1572872 | tf_op jit(solution)/shard_map/ppermute | solution.py:31
  5.4 24.0 %collective-permute-start.17 = (bf16[512,512]{1,0:T(8,128)(2,1)S(1)}, bf16[512,512]{1,0:T(8,128)(2,1)S(1)}, u32[]{:S(2)}, u32[]{:S(2)}) collective-permute-start(bf16[512,512]{1,0:T(8,128)(2,1)S(1)} %shard_map.89.zero.refs_8_.refs_4_), channel_id=1, source_target_pairs={{0,18},{1,19},{2,16},{3,17},{16,2},{17,3},{18,0},{19,1},{4,22},{5,... | collective-permute-start | bytes 1572872 | tf_op jit(solution)/shard_map/ppermute | solution.py:31
  29.6 50.6 %collective-permute-start.18 = (bf16[4,512,512]{2,1,0:T(8,128)(2,1)S(1)}, bf16[4,512,512]{2,1,0:T(8,128)(2,1)S(1)}, u32[]{:S(2)}, u32[]{:S(2)}) collective-permute-start(bf16[4,512,512]{2,1,0:T(8,128)(2,1)S(1)} %shard_map.90), channel_id=1, source_target_pairs={{0,1},{1,0},{2,3},{3,2},{16,17},{17,16},{18,19},{19,18},{4,5},{5,4... | collective-permute-start | bytes 6291464 | tf_op jit(solution)/shard_map/ppermute | solution.py:31
  39.4 11.6 %collective-permute-start.8 = (bf16[1024,128]{1,0:T(8,128)(2,1)S(1)}, bf16[1024,128]{1,0:T(8,128)(2,1)S(1)}, u32[]{:S(2)}, u32[]{:S(2)}) collective-permute-start(bf16[1024,128]{1,0:T(8,128)(2,1)S(1)} %shard_map.88.refs_1_.refs_8_), channel_id=1, source_target_pairs={{0,32},{32,0},{64,96},{96,64},{128,160},{160,128},{192,224},{224,1... | collective-permute-start | bytes 786440 | tf_op jit(solution)/shard_map/ppermute | solution.py:43
  43.0 13.1 %collective-permute-start.2 = (bf16[1024,128]{1,0:T(8,128)(2,1)S(1)}, bf16[1024,128]{1,0:T(8,128)(2,1)S(1)}, u32[]{:S(2)}, u32[]{:S(2)}) collective-permute-start(bf16[1024,128]{1,0:T(8,128)(2,1)S(1)} %shard_map.87.refs_0_), channel_id=1, source_target_pairs={{0,224},{32,64},{64,32},{96,128},{128,96},{160,192},{192,160},{224... | collective-permute-start | bytes 786440 | tf_op jit(solution)/shard_map/ppermute | solution.py:43
  49.0 12.8 %collective-permute-start.12 = (bf16[1024,128]{1,0:T(8,128)(2,1)S(1)}, bf16[1024,128]{1,0:T(8,128)(2,1)S(1)}, u32[]{:S(2)}, u32[]{:S(2)}) collective-permute-start(bf16[1024,128]{1,0:T(8,128)(2,1)S(1)} %shard_map.88.refs_1_.refs_8_), channel_id=1, source_target_pairs={{0,224},{32,64},{64,32},{96,128},{128,96},{160,192},{192,160},{224... | collective-permute-start | bytes 786440 | tf_op jit(solution)/shard_map/ppermute | solution.py:43
  51.0 16.4 %collective-permute-start.9 = (bf16[1024,128]{1,0:T(8,128)(2,1)S(1)}, bf16[1024,128]{1,0:T(8,128)(2,1)S(1)}, u32[]{:S(2)}, u32[]{:S(2)}) collective-permute-start(bf16[1024,128]{1,0:T(8,128)(2,1)S(1)} %collective-permute-done.8.refs_3_.refs_9_), channel_id=1, source_target_pairs={{0,224},{32,64},{64,32},{96,128},{128,96},{160,192},{192,160},{224... | collective-permute-start | bytes 786440 | tf_op jit(solution)/shard_map/ppermute | solution.py:43
  56.1 11.2 %collective-permute-start.3 = (bf16[1024,128]{1,0:T(8,128)(2,1)S(1)}, bf16[1024,128]{1,0:T(8,128)(2,1)S(1)}, u32[]{:S(2)}, u32[]{:S(2)}) collective-permute-start(bf16[1024,128]{1,0:T(8,128)(2,1)S(1)} %collective-permute-done.2.refs_6_.refs_3_), channel_id=1, source_target_pairs={{0,32},{32,0},{64,96},{96,64},{128,160},{160,128},{192,224},{224,1... | collective-permute-start | bytes 786440 | tf_op jit(solution)/shard_map/ppermute | solution.py:43
  56.1 16.8 %collective-permute-start.20 = (bf16[1024,128]{1,0:T(8,128)(2,1)S(1)}, bf16[1024,128]{1,0:T(8,128)(2,1)S(1)}, u32[]{:S(2)}, u32[]{:S(2)}) collective-permute-start(bf16[1024,128]{1,0:T(8,128)(2,1)S(1)} %collective-permute-done.19.refs_2_.refs_1_), channel_id=1, source_target_pairs={{0,224},{32,64},{64,32},{96,128},{128,96},{160,192},{192,160},{224... | collective-permute-start | bytes 786440 | tf_op jit(solution)/shard_map/ppermute | solution.py:43
  61.7 12.1 %collective-permute-start.13 = (bf16[1024,128]{1,0:T(8,128)(2,1)S(1)}, bf16[1024,128]{1,0:T(8,128)(2,1)S(1)}, u32[]{:S(2)}, u32[]{:S(2)}) collective-permute-start(bf16[1024,128]{1,0:T(8,128)(2,1)S(1)} %collective-permute-done.12.refs_7_.refs_11_), channel_id=1, source_target_pairs={{0,32},{32,0},{64,96},{96,64},{128,160},{160,128},{192,224},{224,1... | collective-permute-start | bytes 786440 | tf_op jit(solution)/shard_map/ppermute | solution.py:43
  67.4 12.4 %collective-permute-start.4 = (bf16[1024,128]{1,0:T(8,128)(2,1)S(1)}, bf16[1024,128]{1,0:T(8,128)(2,1)S(1)}, u32[]{:S(2)}, u32[]{:S(2)}) collective-permute-start(bf16[1024,128]{1,0:T(8,128)(2,1)S(1)} %collective-permute-done.3.refs_0_.refs_4_), channel_id=1, source_target_pairs={{0,224},{32,64},{64,32},{96,128},{128,96},{160,192},{192,160},{224... | collective-permute-start | bytes 786440 | tf_op jit(solution)/shard_map/ppermute | solution.py:43
  73.8 20.7 %collective-permute-start.25 = (bf16[2,512,128]{2,1,0:T(8,128)(2,1)S(1)}, bf16[2,512,128]{2,1,0:T(8,128)(2,1)S(1)}, u32[]{:S(2)}, u32[]{:S(2)}) collective-permute-start(bf16[2,512,128]{2,1,0:T(8,128)(2,1)S(1)} %get-tuple-element.49), channel_id=1, source_target_pairs={{0,2},{1,3},{2,0},{3,1},{16,18},{17,19},{18,16},{19,17},{4,6},{5,7... | collective-permute-start | bytes 786440 | tf_op jit(solution)/shard_map/ppermute | solution.py:31
  89.7 17.9 %collective-permute-start.22 = (bf16[2,512,256]{2,1,0:T(8,128)(2,1)S(1)}, bf16[2,512,256]{2,1,0:T(8,128)(2,1)S(1)}, u32[]{:S(2)}, u32[]{:S(2)}) collective-permute-start(bf16[2,512,256]{2,1,0:T(8,128)(2,1)S(1)} %get-tuple-element.45), channel_id=1, source_target_pairs={{0,4},{4,0},{8,12},{12,8},{1,5},{5,1},{9,13},{13,9},{2,6},{6,2},{1... | collective-permute-start | bytes 1572872 | tf_op jit(solution)/shard_map/ppermute | solution.py:47
  91.4 21.1 %collective-permute-start.23 = (bf16[2,512,256]{2,1,0:T(8,128)(2,1)S(1)}, bf16[2,512,256]{2,1,0:T(8,128)(2,1)S(1)}, u32[]{:S(2)}, u32[]{:S(2)}) collective-permute-start(bf16[2,512,256]{2,1,0:T(8,128)(2,1)S(1)} %get-tuple-element.46), channel_id=1, source_target_pairs={{0,8},{4,12},{8,0},{12,4},{1,9},{5,13},{9,1},{13,5},{2,10},{6,14},... | collective-permute-start | bytes 1572872 | tf_op jit(solution)/shard_map/ppermute | solution.py:47
  94.3 20.9 %collective-permute-start.24 = (bf16[2,512,256]{2,1,0:T(8,128)(2,1)S(1)}, bf16[2,512,256]{2,1,0:T(8,128)(2,1)S(1)}, u32[]{:S(2)}, u32[]{:S(2)}) collective-permute-start(bf16[2,512,256]{2,1,0:T(8,128)(2,1)S(1)} %get-tuple-element.47), channel_id=1, source_target_pairs={{0,12},{4,8},{8,4},{12,0},{1,13},{5,9},{9,5},{13,1},{2,14},{6,10},... | collective-permute-start | bytes 1572872 | tf_op jit(solution)/shard_map/ppermute | solution.py:47
  94.5 13.1 %collective-permute-start.27 = (bf16[2,512,128]{2,1,0:T(8,128)(2,1)S(1)}, bf16[2,512,128]{2,1,0:T(8,128)(2,1)S(1)}, u32[]{:S(2)}, u32[]{:S(2)}) collective-permute-start(bf16[2,512,128]{2,1,0:T(8,128)(2,1)S(1)} %get-tuple-element.51), channel_id=1, source_target_pairs={{0,18},{1,19},{2,16},{3,17},{16,2},{17,3},{18,0},{19,1},{4,22},{5,... | collective-permute-start | bytes 786440 | tf_op jit(solution)/shard_map/ppermute | solution.py:31
  117.4 16.1 %collective-permute-start.40 = (bf16[2,256,256]{2,1,0:T(8,128)(2,1)S(1)}, bf16[2,256,256]{2,1,0:T(8,128)(2,1)S(1)}, u32[]{:S(2)}, u32[]{:S(2)}) collective-permute-start(bf16[2,256,256]{2,1,0:T(8,128)(2,1)S(1)} %get-tuple-element.57.refs_0_), channel_id=1, source_target_pairs={{0,16},{1,17},{2,18},{3,19},{16,0},{17,1},{18,2},{19,3},{4,20},{5,... | collective-permute-start | bytes 786440 | tf_op jit(solution)/shard_map/ppermute | solution.py:31
  120.9 14.8 %collective-permute-start.41 = (bf16[2,256,256]{2,1,0:T(8,128)(2,1)S(1)}, bf16[2,256,256]{2,1,0:T(8,128)(2,1)S(1)}, u32[]{:S(2)}, u32[]{:S(2)}) collective-permute-start(bf16[2,256,256]{2,1,0:T(8,128)(2,1)S(1)} %get-tuple-element.57.refs_0_), channel_id=1, source_target_pairs={{0,18},{1,19},{2,16},{3,17},{16,2},{17,3},{18,0},{19,1},{4,22},{5,... | collective-permute-start | bytes 786440 | tf_op jit(solution)/shard_map/ppermute | solution.py:31
  120.9 15.0 %collective-permute-start.31 = (bf16[2,256,256]{2,1,0:T(8,128)(2,1)S(1)}, bf16[2,256,256]{2,1,0:T(8,128)(2,1)S(1)}, u32[]{:S(2)}, u32[]{:S(2)}) collective-permute-start(bf16[2,256,256]{2,1,0:T(8,128)(2,1)S(1)} %get-tuple-element.56.refs_0_), channel_id=1, source_target_pairs={{0,2},{1,3},{2,0},{3,1},{16,18},{17,19},{18,16},{19,17},{4,6},{5,7... | collective-permute-start | bytes 786440 | tf_op jit(solution)/shard_map/ppermute | solution.py:31
  122.3 22.5 %collective-permute-start.32 = (bf16[2,256,256]{2,1,0:T(8,128)(2,1)S(1)}, bf16[2,256,256]{2,1,0:T(8,128)(2,1)S(1)}, u32[]{:S(2)}, u32[]{:S(2)}) collective-permute-start(bf16[2,256,256]{2,1,0:T(8,128)(2,1)S(1)} %get-tuple-element.56.refs_0_), channel_id=1, source_target_pairs={{0,16},{1,17},{2,18},{3,19},{16,0},{17,1},{18,2},{19,3},{4,20},{5,... | collective-permute-start | bytes 786440 | tf_op jit(solution)/shard_map/ppermute | solution.py:31
  124.4 22.3 %collective-permute-start.33 = (bf16[2,256,256]{2,1,0:T(8,128)(2,1)S(1)}, bf16[2,256,256]{2,1,0:T(8,128)(2,1)S(1)}, u32[]{:S(2)}, u32[]{:S(2)}) collective-permute-start(bf16[2,256,256]{2,1,0:T(8,128)(2,1)S(1)} %get-tuple-element.56.refs_0_), channel_id=1, source_target_pairs={{0,18},{1,19},{2,16},{3,17},{16,2},{17,3},{18,0},{19,1},{4,22},{5,... | collective-permute-start | bytes 786440 | tf_op jit(solution)/shard_map/ppermute | solution.py:31
  135.8 14.3 %collective-permute-start.43 = (bf16[3,2,256,256]{3,2,1,0:T(8,128)(2,1)S(1)}, bf16[3,2,256,256]{3,2,1,0:T(8,128)(2,1)S(1)}, u32[]{:S(2)}, u32[]{:S(2)}) collective-permute-start(bf16[3,2,256,256]{3,2,1,0:T(8,128)(2,1)S(1)} %shard_map.97), channel_id=1, source_target_pairs={{0,1},{1,0},{2,3},{3,2},{16,17},{17,16},{18,19},{19,18},{4,5},{5,4... | collective-permute-start | bytes 2359304 | tf_op jit(solution)/shard_map/ppermute | solution.py:31
  146.8 11.4 %collective-permute-start.35 = (bf16[3,2,256,256]{3,2,1,0:T(8,128)(2,1)S(1)}, bf16[3,2,256,256]{3,2,1,0:T(8,128)(2,1)S(1)}, u32[]{:S(2)}, u32[]{:S(2)}) collective-permute-start(bf16[3,2,256,256]{3,2,1,0:T(8,128)(2,1)S(1)} %shard_map.95), channel_id=1, source_target_pairs={{0,1},{1,0},{2,3},{3,2},{16,17},{17,16},{18,19},{19,18},{4,5},{5,4... | collective-permute-start | bytes 2359304 | tf_op jit(solution)/shard_map/ppermute | solution.py:31
  151.3 16.1 %collective-permute-start.46 = (bf16[2,256,256]{2,1,0:T(8,128)(2,1)S(1)}, bf16[2,256,256]{2,1,0:T(8,128)(2,1)S(1)}, u32[]{:S(2)}, u32[]{:S(2)}) collective-permute-start(bf16[2,256,256]{2,1,0:T(8,128)(2,1)S(1)} %second.15), channel_id=1, source_target_pairs={{0,12},{4,8},{8,4},{12,0},{1,13},{5,9},{9,5},{13,1},{2,14},{6,10},... | collective-permute-start | bytes 786440 | tf_op jit(solution)/shard_map/ppermute | solution.py:47
  152.9 14.6 %collective-permute-start.45 = (bf16[2,256,256]{2,1,0:T(8,128)(2,1)S(1)}, bf16[2,256,256]{2,1,0:T(8,128)(2,1)S(1)}, u32[]{:S(2)}, u32[]{:S(2)}) collective-permute-start(bf16[2,256,256]{2,1,0:T(8,128)(2,1)S(1)} %second.14), channel_id=1, source_target_pairs={{0,8},{4,12},{8,0},{12,4},{1,9},{5,13},{9,1},{13,5},{2,10},{6,14},... | collective-permute-start | bytes 786440 | tf_op jit(solution)/shard_map/ppermute | solution.py:47
  155.0 17.7 %collective-permute-start.44 = (bf16[2,256,256]{2,1,0:T(8,128)(2,1)S(1)}, bf16[2,256,256]{2,1,0:T(8,128)(2,1)S(1)}, u32[]{:S(2)}, u32[]{:S(2)}) collective-permute-start(bf16[2,256,256]{2,1,0:T(8,128)(2,1)S(1)} %second.13), channel_id=1, source_target_pairs={{0,4},{4,0},{8,12},{12,8},{1,5},{5,1},{9,13},{13,9},{2,6},{6,2},{1... | collective-permute-start | bytes 786440 | tf_op jit(solution)/shard_map/ppermute | solution.py:47
  159.5 18.4 %collective-permute-start.38 = (bf16[2,256,256]{2,1,0:T(8,128)(2,1)S(1)}, bf16[2,256,256]{2,1,0:T(8,128)(2,1)S(1)}, u32[]{:S(2)}, u32[]{:S(2)}) collective-permute-start(bf16[2,256,256]{2,1,0:T(8,128)(2,1)S(1)} %second.11), channel_id=1, source_target_pairs={{0,12},{4,8},{8,4},{12,0},{1,13},{5,9},{9,5},{13,1},{2,14},{6,10},... | collective-permute-start | bytes 786440 | tf_op jit(solution)/shard_map/ppermute | solution.py:47
  161.1 17.0 %collective-permute-start.37 = (bf16[2,256,256]{2,1,0:T(8,128)(2,1)S(1)}, bf16[2,256,256]{2,1,0:T(8,128)(2,1)S(1)}, u32[]{:S(2)}, u32[]{:S(2)}) collective-permute-start(bf16[2,256,256]{2,1,0:T(8,128)(2,1)S(1)} %second.10), channel_id=1, source_target_pairs={{0,8},{4,12},{8,0},{12,4},{1,9},{5,13},{9,1},{13,5},{2,10},{6,14},... | collective-permute-start | bytes 786440 | tf_op jit(solution)/shard_map/ppermute | solution.py:47
  167.4 12.5 %collective-permute-start.36 = (bf16[2,256,256]{2,1,0:T(8,128)(2,1)S(1)}, bf16[2,256,256]{2,1,0:T(8,128)(2,1)S(1)}, u32[]{:S(2)}, u32[]{:S(2)}) collective-permute-start(bf16[2,256,256]{2,1,0:T(8,128)(2,1)S(1)} %second.9), channel_id=1, source_target_pairs={{0,4},{4,0},{8,12},{12,8},{1,5},{5,1},{9,13},{13,9},{2,6},{6,2},{1... | collective-permute-start | bytes 786440 | tf_op jit(solution)/shard_map/ppermute | solution.py:47
  167.4 16.3 %collective-permute-start.28 = (bf16[512,128]{1,0:T(8,128)(2,1)S(1)}, bf16[512,128]{1,0:T(8,128)(2,1)S(1)}, u32[]{:S(2)}, u32[]{:S(2)}) collective-permute-start(bf16[512,128]{1,0:T(8,128)(2,1)S(1)} %get-tuple-element.53), channel_id=1, source_target_pairs={{0,2},{1,3},{2,0},{3,1},{16,18},{17,19},{18,16},{19,17},{4,6},{5,7... | collective-permute-start | bytes 393224 | tf_op jit(solution)/shard_map/ppermute | solution.py:31
  172.7 12.4 %collective-permute-start.29 = (bf16[512,128]{1,0:T(8,128)(2,1)S(1)}, bf16[512,128]{1,0:T(8,128)(2,1)S(1)}, u32[]{:S(2)}, u32[]{:S(2)}) collective-permute-start(bf16[512,128]{1,0:T(8,128)(2,1)S(1)} %get-tuple-element.54), channel_id=1, source_target_pairs={{0,16},{1,17},{2,18},{3,19},{16,0},{17,1},{18,2},{19,3},{4,20},{5,... | collective-permute-start | bytes 393224 | tf_op jit(solution)/shard_map/ppermute | solution.py:31
  (23 other events, 326.8 us)
